TPU v7x, 256 devices: a whole 4x4x8 slice. The times are simulated.
256 devices in a mesh: dp: 8 (over y, core), tile: 32 (over x, z).
Axes of the slice: x: 4, y: 4, z: 8, core: 2. Of those that a mesh axis runs over, the one named last changes fastest.
Arguments:
- video_in: bfloat16 [8, 64, 128, 8, 256], P('dp', None, 'tile'), may hold values from -12 to 12
- clip_lengths: int32 [8, 6], P('dp'), may hold values from 1 to 21, 64 in all within a row
- norm_gain: float32 [256], replicated, may hold values from 0.1 to 1.9
- norm_bias: float32 [256], replicated, may hold values from -3 to 3
- spatial_weight: bfloat16 [3, 3, 256, 256], replicated, may hold values from -0.125 to 0.125
- temporal_weight: bfloat16 [3, 256, 256], replicated, may hold values from -0.21875 to 0.21875
- cotangent: bfloat16 [8, 64, 128, 8, 256], P('dp', 'tile'), may hold values from -6 to 6
Outputs:
- encoded: bfloat16 [8, 64, 128, 8, 256], P('dp', 'tile')
- spatial_grad: float32 [3, 3, 256, 256], replicated
- temporal_grad: float32 [3, 256, 256], replicated
Inputs may be any that keep to these rules, and one draw needn't show every extreme that they name: `clip_lengths`: the lengths of each batch sum to 64.
All inputs are finite; a program needn't handle non-finite values.
Results may differ from a plain program's by a relative error of at most 0.005.
Values may be sent and summed in bfloat16 or wider, within the bound.
No kernel may reach another device: no remote copies, remote signals or barrier semaphores. Data moves between devices by JAX's collectives and lax.ppermute only.
A program may use at most 64 MiB of HBM per device.

v0:
```python
import functools
import math

import jax
import jax.numpy as jnp
from jax import lax
from jax.sharding import Mesh
from jax.sharding import PartitionSpec as P

GROUPS = 32
TILE = ("tile_0", "tile_1")
DP_TILE = ("dp", "tile_0", "tile_1")


norm_eps = 1e-05


def by_axis(shard, axes):
    return functools.reduce(lax.psum, axes, shard)


def extended(cells, sides, width):
    for axis, dim in sides:
        count = lax.axis_size(axis)
        ends = count - 1
        head = lax.slice_in_dim(cells, 0, width, axis=dim)
        tail = lax.slice_in_dim(cells, cells.shape[dim] - width, cells.shape[dim], axis=dim)
        cells = jnp.concatenate(
            [
                lax.ppermute(tail, axis, [(i, (i + 1) % count) for i in range(ends)]),
                cells,
                lax.ppermute(head, axis, [((i + 1) % count, i) for i in range(ends)]),
            ],
            axis=dim,
        )
    return cells


def clip_tables(lengths, frame_total):
    clip_ends = jnp.cumsum(lengths)
    clip_starts = clip_ends - lengths
    frame_ids = jnp.arange(frame_total, dtype=jnp.int32)
    membership = (frame_ids[:, None] >= clip_starts[None, :]) & (
        frame_ids[:, None] < clip_ends[None, :]
    )
    clip_first = jnp.sum(jnp.where(membership, clip_starts[None, :], 0), axis=1)
    return (membership.astype(jnp.float32), frame_ids - clip_first)


def group_total(onehot, frame_term, group_count):
    clip_term = jnp.dot(onehot.T, frame_term, precision=lax.Precision.HIGHEST)
    return clip_term.reshape(clip_term.shape[0], group_count, -1).sum(axis=2)


def spread_back(onehot, clip_group, channels):
    per_channel = jnp.repeat(clip_group, channels // clip_group.shape[1], axis=1)
    return jnp.dot(onehot, per_channel, precision=lax.Precision.HIGHEST)


def patch_columns(padded, strip_rows, frame_width):
    pieces = [
        padded[:, row_step : row_step + strip_rows, col_step : col_step + frame_width, :]
        for row_step in range(3)
        for col_step in range(3)
    ]
    return jnp.concatenate(pieces, axis=-1).reshape(-1, 9 * padded.shape[-1])


def earlier_stack(block_ext, pos_here):
    frame_count = pos_here.shape[0]
    stacked = []
    for offset in range(3):
        keep = (pos_here >= offset)[:, None, None, None]
        window = block_ext[2 - offset : 2 - offset + frame_count]
        stacked.append(jnp.where(keep, window, jnp.zeros_like(window)))
    return jnp.concatenate(stacked, axis=-1)


def later_stack(cot_ext, pos_ahead):
    frame_count = pos_ahead.shape[0] - 2
    stacked = []
    for offset in range(3):
        keep = (pos_ahead[offset : offset + frame_count] >= offset)[:, None, None, None]
        window = cot_ext[offset : offset + frame_count]
        stacked.append(jnp.where(keep, window, jnp.zeros_like(window)))
    return jnp.concatenate(stacked, axis=-1)


def contract_rows(left, right):
    return lax.dot_general(
        left, right, (((0,), (0,)), ((), ())), preferred_element_type=jnp.float32
    )


def temporal_pass(block_ext, cot_ext, pos_here, pos_ahead, temporal_weight):
    channels = temporal_weight.shape[1]
    frame_count = pos_here.shape[0]
    earlier = earlier_stack(block_ext, pos_here).reshape(-1, 3 * channels)
    block_now = block_ext[2:]
    lifted = jnp.dot(
        earlier, temporal_weight.reshape(3 * channels, channels), preferred_element_type=jnp.float32
    )
    encoded = (block_now.astype(jnp.float32) + lifted.reshape(block_now.shape)).astype(jnp.bfloat16)
    cot_now = cot_ext[:frame_count]
    later_cot = later_stack(cot_ext, pos_ahead).reshape(-1, 3 * channels)
    back_weight = jnp.transpose(temporal_weight, (0, 2, 1)).reshape(3 * channels, channels)
    pulled = jnp.dot(later_cot, back_weight, preferred_element_type=jnp.float32)
    grad_block = (cot_now.astype(jnp.float32) + pulled.reshape(cot_now.shape)).astype(jnp.bfloat16)
    temporal_term = contract_rows(earlier, cot_now.reshape(-1, channels))
    return (encoded, grad_block, temporal_term)


def on_device(
    video_in, clip_lengths, norm_gain, norm_bias, spatial_weight, temporal_weight, cotangent
):
    tile_count = lax.axis_size(TILE)
    frames = video_in.shape[1]
    strip_rows = video_in.shape[2]
    frame_width = video_in.shape[3]
    channels = video_in.shape[4]
    height = strip_rows * tile_count
    lengths = clip_lengths[0]
    onehot, position = clip_tables(lengths, frames)
    local_vals = video_in[0].astype(jnp.float32)
    per_group = channels // GROUPS
    counts = lengths.astype(jnp.float32) * (height * frame_width * per_group)
    frame_sum = jnp.sum(local_vals, axis=(1, 2))
    totals, squares = (
        by_axis(group_total(onehot, frame_sum, GROUPS), TILE),
        by_axis(group_total(onehot, jnp.sum(local_vals * local_vals, axis=(1, 2)), GROUPS), TILE),
    )
    clip_mean = totals / counts[:, None]
    clip_var = squares / counts[:, None] - clip_mean * clip_mean
    centered = local_vals - spread_back(onehot, clip_mean, channels)[:, None, None, :]
    rstd_frame = spread_back(onehot, lax.rsqrt(clip_var + norm_eps), channels)
    normed = centered * rstd_frame[:, None, None, :] * norm_gain + norm_bias
    active = jax.nn.silu(normed).astype(jnp.bfloat16)
    padded = extended(active, ((TILE, 1),), 1)
    padded = jnp.pad(padded, ((0, 0), (0, 0), (1, 1), (0, 0)))
    columns = patch_columns(padded, strip_rows, frame_width)
    conv_out = jnp.dot(
        columns, spatial_weight.reshape(9 * channels, channels), preferred_element_type=jnp.float32
    )
    block_out = (local_vals + conv_out.reshape(local_vals.shape)).astype(jnp.bfloat16)
    cot_rows = lax.all_to_all(cotangent, TILE, split_axis=2, concat_axis=1, tiled=True)[0]
    blank_frames = jnp.zeros((2, strip_rows, frame_width, channels), jnp.bfloat16)
    block_ext = jnp.concatenate([blank_frames, block_out], axis=0)
    cot_ext = jnp.concatenate([cot_rows, blank_frames], axis=0)
    pos_ahead = jnp.concatenate([position, jnp.zeros((2,), jnp.int32)], axis=0)
    encoded_rows, grad_block, temporal_term = temporal_pass(
        block_ext, cot_ext, position, pos_ahead, temporal_weight
    )
    encoded = lax.all_to_all(encoded_rows[None], TILE, split_axis=1, concat_axis=2, tiled=True)
    spatial_term = contract_rows(columns, grad_block.reshape(-1, channels))
    pixel_total = lax.axis_size("dp") * frames * height * frame_width
    grad_scale = 1.0 / math.sqrt(pixel_total)
    spatial_grad, temporal_grad = lax.psum(
        (spatial_term * grad_scale, temporal_term * grad_scale), DP_TILE
    )
    return (
        encoded,
        spatial_grad.reshape(3, 3, channels, channels),
        temporal_grad.reshape(3, channels, channels),
    )


def solution(mesh):
    finer = Mesh(mesh.devices.reshape(mesh.shape["dp"], 4, 8), ("dp", "tile_0", "tile_1"))
    in_specs = (
        P("dp", None, TILE, None, None),
        P("dp", None),
        P(),
        P(),
        P(),
        P(),
        P("dp", TILE, None, None, None),
    )
    out_specs = (P("dp", TILE, None, None, None), P(), P())
    return jax.shard_map(
        on_device, mesh=finer, in_specs=in_specs, out_specs=out_specs, check_vma=False
    )
```

profile of v0, /device:TPU:2, one launch (start us, length us, event | category | flops | bytes accessed | tf_op | source)
XLA Modules:
  0.0 393.7 jit_solution(4188990313821807785)
XLA Ops:
  7.2 1.7 convert_reduce_fusion
  8.9 1.6 fusion.25
  10.5 0.7 multiply_bitcast_fusion
  11.2 0.8 reduce-window.4
  12.0 0.7 fusion.37
  12.8 0.4 convolution_reduce_fusion.1
  13.2 0.4 convolution_reduce_fusion
  13.6 10.1 %all-reduce.6 = (f32[6,32]{1,0:T(8,128)S(1)}, f32[6,32]{1,0:T(8,128)S(1)}) all-reduce(f32[6,32]{1,0:T(8,128)S(1)} %convolution_reduce_fusion, f32[6,32]{1,0:T(8,128)S(1)} %convolution_reduce_fusion.1), channel_id=1, replica_groups=mesh['dp'=8,'tile_0'=4,'tile_1'=8] {'tile_0'}, use_global_device_ids=true, to_apply=%region_7.8 | all-reduce | flops 384 | bytes 3072 | tf_op jit(solution)/shard_map/psum | solution.py:19
  23.7 18.9 %all-reduce.5 = (f32[6,32]{1,0:T(8,128)S(1)}, f32[6,32]{1,0:T(8,128)S(1)}) all-reduce(f32[6,32]{1,0:T(8,128)S(1)} %get-tuple-element.7, f32[6,32]{1,0:T(8,128)S(1)} %get-tuple-element.8), channel_id=1, replica_groups=mesh['dp'=8,'tile_0'=4,'tile_1'=8] {'tile_1'}, use_global_device_ids=true, to_apply=%region_8.9 | all-reduce | flops 384 | bytes 3072 | tf_op jit(solution)/shard_map/psum | solution.py:19
  42.8 0.1 reshape.93
  42.9 0.3 fusion.42
  43.4 0.3 fusion.40
  43.8 0.7 fusion.24
  44.5 0.8 fusion.45
  45.4 1.9 collective-permute-start
  47.3 6.0 %collective-permute-start.1 = (bf16[64,1,8,256]{3,2,1,0:T(8,128)(2,1)}, bf16[64,1,8,256]{3,2,1,0:T(8,128)(2,1)S(1)}, u32[]{:S(2)}, u32[]{:S(2)}) collective-permute-start(bf16[64,1,8,256]{3,2,1,0:T(8,128)(2,1)} %get-tuple-element.15), channel_id=1, source_target_pairs={{1,0},{2,1},{3,2},{4,3},{5,4},{6,5},{7,6},{8,7},{9,8},{10,9},{11,1... | collective-permute-start | bytes 786440 | tf_op jit(solution)/shard_map/ppermute | solution.py:32
  53.3 2.3 copy.27
  55.6 5.6 %all-to-all-start.1 = ((bf16[1,2,128,8,256]{4,3,1,0,2:T(8,128)(2,1)}), bf16[1,2,128,8,256]{4,3,1,0,2:T(8,128)(2,1)}, u32[]{:S(2)}, u32[]{:S(2)}) async-start(bf16[1,2,128,8,256]{4,3,1,0,2:T(8,128)(2,1)} %copy.27), calls=%async_computation.1 | async-start | bytes 2097152 | tf_op jit(solution)/shard_map/all_to_all | solution.py:145
  61.4 0.5 copy-done.18
  61.9 0.7 slice_compare_fusion.1
  62.6 1.9 copy.29
  64.5 1.1 broadcast_compare_fusion.2
  65.6 1.5 collective-permute-done.1
  67.1 2.5 fusion.6
  69.6 1.1 fusion.31
  70.7 0.3 slice_dynamic-update-slice_fusion.4
  71.2 0.8 constant_dynamic-update-slice_fusion
  71.9 0.3 slice_dynamic-update-slice_fusion.2
  72.4 0.3 slice_dynamic-update-slice_fusion
  72.8 3.6 copy-done.12
  76.4 3.7 fusion.26
  80.1 0.6 all-to-all-done.1
  80.8 1.3 copy.28
  82.2 3.3 broadcast_select_fusion.1
  85.5 0.9 copy-done.3
  86.5 0.4 copy-done.4
  86.8 2.0 fusion.29
  88.8 9.7 %all-to-all-start = ((bf16[1,64,4,8,256]{4,3,2,0,1:T(8,128)(2,1)}), bf16[1,64,4,8,256]{4,3,2,0,1:T(8,128)(2,1)S(1)}, u32[]{:S(2)}, u32[]{:S(2)}) async-start(bf16[1,64,4,8,256]{4,3,2,0,1:T(8,128)(2,1)} %fusion.29), calls=%async_computation | async-start | bytes 2097152 | tf_op jit(solution)/shard_map/all_to_all | solution.py:153
  98.5 0.2 all-reduce.9.cloned.1.call-start
  98.8 1.5 slice_select_fusion.1
  100.3 10.8 %fusion.1 = f32[2304,256]{1,0:T(8,128)} fusion(bf16[64,4,8,2304]{3,2,1,0:T(8,128)(2,1)} %copy-done.12, bf16[64,4,8,256]{3,2,1,0:T(8,128)(2,1)S(1)} %bitcast.110, bf16[768,256,1,1]{1,0,3,2:T(8,128)(2,1)} %bitcast.120, bf16[64,4,8,256]{3,2,1,0:T(8,128)(2,1)} %get-tuple-element.10, bf16[64,4,8,256]{3,2,1,0:T(8,128)(2,1)} %get-tuple-element.9, ...), kind=kOutput, calls=%fused_computation.4 | convolution fusion | flops 3232825344 | bytes 16384000 | tf_op jit(solution)/shard_map/dot_general | solution.py:90
  111.1 2.0 pad_maximum_fusion
  113.1 1.9 convolution_multiply_fusion
  115.0 5.6 %all-to-all-done = bf16[1,64,4,8,256]{4,3,2,0,1:T(8,128)(2,1)S(1)} async-done(((bf16[1,64,4,8,256]{4,3,2,0,1:T(8,128)(2,1)}), bf16[1,64,4,8,256]{4,3,2,0,1:T(8,128)(2,1)S(1)}, u32[]{:S(2)}, u32[]{:S(2)}) %all-to-all-start) | async-done | bytes 1048608 | tf_op jit(solution)/shard_map/all_to_all | solution.py:153
  120.6 1.1 copy.26
  121.7 261.0 %all-reduce.9.cloned.1.call-done = (f32[3,3,256,256]{3,2,1,0:T(8,128)}, f32[3,256,256]{2,1,0:T(8,128)}) async-done(((f32[3,3,256,256]{3,2,1,0:T(8,128)}, f32[3,256,256]{2,1,0:T(8,128)}), (f32[3,3,256,256]{3,2,1,0:T(8,128)}, f32[3,256,256]{2,1,0:T(8,128)})) %all-reduce.9.cloned.1.call-update) | async-done | bytes 3145744 | tf_op jit(solution)/shard_map/psum | solution.py:157
  382.7 3.3 copy.48
  386.0 0.9 copy.49
  (48 shorter events, 1.0 us)
Async XLA Ops:
  7.2 65.6 %copy-start = (bf16[3,3,256,256]{3,2,1,0:T(8,128)(2,1)S(1)}, bf16[3,3,256,256]{3,2,1,0:T(8,128)(2,1)}, u32[]{:S(2)}) copy-start(bf16[3,3,256,256]{3,2,1,0:T(8,128)(2,1)} %param.11) | copy-start | bytes 3538948
  7.2 36.6 %copy-start.1 = (bf16[1,64,4,8,256]{4,3,2,1,0:T(8,128)(2,1)S(1)}, bf16[1,64,4,8,256]{4,3,2,1,0:T(8,128)(2,1)}, u32[]{:S(2)}) copy-start(bf16[1,64,4,8,256]{4,3,2,1,0:T(8,128)(2,1)} %param.7) | copy-start | bytes 3145732
  7.2 36.6 %copy-start.13 = (f32[256]{0:T(256)S(1)}, f32[256]{0:T(256)}, u32[]{:S(2)}) copy-start(f32[256]{0:T(256)} %param.10) | copy-start | bytes 3076
  7.2 36.6 %copy-start.14 = (f32[256]{0:T(256)S(1)}, f32[256]{0:T(256)}, u32[]{:S(2)}) copy-start(f32[256]{0:T(256)} %param.9) | copy-start | bytes 3076
  43.2 4.0 %copy-start.8 = (f32[64,256]{1,0:T(8,128)}, f32[64,256]{1,0:T(8,128)S(1)}, u32[]{:S(2)}) copy-start(f32[64,256]{1,0:T(8,128)S(1)} %fusion.42) | copy-start | bytes 196612
  43.8 3.5 copy-start.10
  45.4 20.2 %collective-permute-start = (bf16[64,1,8,256]{3,2,1,0:T(8,128)(2,1)}, bf16[64,1,8,256]{3,2,1,0:T(8,128)(2,1)}, u32[]{:S(2)}, u32[]{:S(2)}) collective-permute-start(bf16[64,1,8,256]{3,2,1,0:T(8,128)(2,1)} %get-tuple-element.14), channel_id=1, source_target_pairs={{0,1},{1,2},{2,3},{3,4},{4,5},{5,6},{6,7},{7,8},{8,9},{9,10},{10,1... | collective-permute-start | bytes 786440 | tf_op jit(solution)/shard_map/ppermute | solution.py:30
  47.3 19.8 %collective-permute-start.1 = (bf16[64,1,8,256]{3,2,1,0:T(8,128)(2,1)}, bf16[64,1,8,256]{3,2,1,0:T(8,128)(2,1)S(1)}, u32[]{:S(2)}, u32[]{:S(2)}) collective-permute-start(bf16[64,1,8,256]{3,2,1,0:T(8,128)(2,1)} %get-tuple-element.15), channel_id=1, source_target_pairs={{1,0},{2,1},{3,2},{4,3},{5,4},{6,5},{7,6},{8,7},{9,8},{10,9},{11,1... | collective-permute-start | bytes 786440 | tf_op jit(solution)/shard_map/ppermute | solution.py:32
  55.6 25.2 %all-to-all-start.1 = ((bf16[1,2,128,8,256]{4,3,1,0,2:T(8,128)(2,1)}), bf16[1,2,128,8,256]{4,3,1,0,2:T(8,128)(2,1)}, u32[]{:S(2)}, u32[]{:S(2)}) async-start(bf16[1,2,128,8,256]{4,3,1,0,2:T(8,128)(2,1)} %copy.27), calls=%async_computation.1 | async-start | bytes 2097152 | tf_op jit(solution)/shard_map/all_to_all | solution.py:145
  61.4 0.5 copy-start.18
  69.6 1.5 copy-start.9
  69.6 1.5 copy-start.11
  72.8 3.6 copy-start.12
  76.4 5.7 %copy-start.15 = (pred[64]{0:T(512)(128)(4,1)S(1)}, pred[64]{0:T(512)(128)(4,1)}, u32[]{:S(2)}) copy-start(pred[64]{0:T(512)(128)(4,1)} %get-tuple-element.23) | copy-start | bytes 196
  82.2 4.7 %copy-start.5 = (bf16[64,4,8,256]{3,2,1,0:T(8,128)(2,1)S(1)}, bf16[64,4,8,256]{3,2,1,0:T(8,128)(2,1)}, u32[]{:S(2)}) copy-start(bf16[64,4,8,256]{3,2,1,0:T(8,128)(2,1)} %fusion.26) | copy-start | bytes 3145732
  82.2 4.6 %copy-start.7 = (bf16[3,256,256]{2,1,0:T(8,128)(2,1)S(1)}, bf16[3,256,256]{2,1,0:T(8,128)(2,1)}, u32[]{:S(2)}) copy-start(bf16[3,256,256]{2,1,0:T(8,128)(2,1)} %param.12) | copy-start | bytes 1179652
  85.5 0.9 copy-start.3
  85.5 1.3 copy-start.4
  85.5 3.3 copy-start.2
  86.8 12.0 %copy-start.16 = (pred[64]{0:T(512)(128)(4,1)S(1)}, pred[64]{0:T(512)(128)(4,1)}, u32[]{:S(2)}) copy-start(pred[64]{0:T(512)(128)(4,1)} %get-tuple-element.19) | copy-start | bytes 196
  86.8 12.0 %copy-start.17 = (pred[64]{0:T(512)(128)(4,1)S(1)}, pred[64]{0:T(512)(128)(4,1)}, u32[]{:S(2)}) copy-start(pred[64]{0:T(512)(128)(4,1)} %get-tuple-element.20) | copy-start | bytes 196
  88.8 31.8 %all-to-all-start = ((bf16[1,64,4,8,256]{4,3,2,0,1:T(8,128)(2,1)}), bf16[1,64,4,8,256]{4,3,2,0,1:T(8,128)(2,1)S(1)}, u32[]{:S(2)}, u32[]{:S(2)}) async-start(bf16[1,64,4,8,256]{4,3,2,0,1:T(8,128)(2,1)} %fusion.29), calls=%async_computation | async-start | bytes 2097152 | tf_op jit(solution)/shard_map/all_to_all | solution.py:153
  98.5 284.2 %all-reduce.9.cloned.1.call-start = ((), (), s32[]{:S(2)}) async-start(), calls=%async_computation.2 | async-start | bytes 6291456 | tf_op jit(solution)/shard_map/psum | solution.py:157
  382.7 3.3 copy-start.6
Sparse Core Ops, SparseCore 0:
  115.2 267.5 all-reduce.8
where the time goes:
time: 394 us
  waiting for transfers between devices  269 us (68%)
  blocking collectives  29 us (7%)
  starting transfers between devices  23.5 us (6%)
  matrix products  19.8 us (5%)
  other arithmetic  19.3 us (5%)
  local copies, waits for them, and re-layouts  18.9 us (5%)
  between operations  14.4 us (4%)
    psum x1, waiting for transfers between devices, on_device(): lax.psum((spatial_term * grad_scale, temporal_term * grad_scale), DP_TILE)  261 us
    psum x2, blocking collectives, by_axis(): return functools.reduce(lax.psum, axes, shard)  29 us
    unnamed x47, local copies, waits for them, and re-layouts  14.8 us
    dot_general x2, matrix products, contract_rows(): lax.dot_general(left, right, (((0,), (0,)), ((), ())), preferred_element_...  12.7 us
    all_to_all x1, starting transfers between devices, on_device(): lax.all_to_all(encoded_rows[None], TILE, split_axis=1, concat_axis=2, til...  9.69 us
  transfers between devices with their start and end apart: 5, of which 4 were waited for; matrix products, arithmetic and copies ran while one was open for 8% of the time, Pallas kernels for 0%

commit v1 on v0

--- a/solution.py
+++ b/solution.py
@@ -1,4 +1,3 @@
-import functools
 import math
 
 import jax
@@ -9,14 +8,43 @@
 
 GROUPS = 32
 TILE = ("tile_0", "tile_1")
-DP_TILE = ("dp", "tile_0", "tile_1")
+DP = ("row", "core")
+MESH_AXES = ("row", "core", "tile_0", "tile_1")
 
 
 norm_eps = 1e-05
 
 
-def by_axis(shard, axes):
-    return functools.reduce(lax.psum, axes, shard)
+def tile_total(part):
+    copies = jnp.broadcast_to(part[None], (lax.axis_size(TILE),) + part.shape)
+    return jnp.sum(lax.all_to_all(copies, TILE, 0, 0, tiled=True), axis=0)
+
+
+def share_sum(parts, axes):
+    count = lax.axis_size(axes)
+    pieces = parts.astype(jnp.bfloat16).reshape((count, -1, parts.shape[-1]))
+    pieces = lax.all_to_all(pieces, axes, 0, 0, tiled=True)
+    return jnp.sum(pieces.astype(jnp.float32), axis=0)
+
+
+def share_copy(piece, axes):
+    copies = jnp.broadcast_to(piece[None], (lax.axis_size(axes),) + piece.shape)
+    return lax.all_to_all(copies, axes, 0, 0, tiled=True).reshape(-1, piece.shape[-1])
+
+
+def total_everywhere(part):
+    swap = [(0, 1), (1, 0)]
+    core = lax.axis_index("core")
+    halves = part.reshape(2, -1, part.shape[-1])
+    other = lax.dynamic_index_in_dim(halves, 1 - core, 0, keepdims=False)
+    mine = lax.dynamic_index_in_dim(halves, core, 0, keepdims=False)
+    mine = mine + lax.ppermute(other.astype(jnp.bfloat16), "core", swap).astype(jnp.float32)
+    piece = share_sum(share_sum(mine, "row"), TILE).astype(jnp.bfloat16)
+    half = share_copy(share_copy(piece, TILE), "row")
+    facing = lax.ppermute(half, "core", swap)
+    first = jnp.where(core == 0, half, facing)
+    second = jnp.where(core == 0, facing, half)
+    return jnp.concatenate([first, second], axis=0).astype(jnp.float32)
 
 
 def extended(cells, sides, width):
@@ -125,9 +153,11 @@
     per_group = channels // GROUPS
     counts = lengths.astype(jnp.float32) * (height * frame_width * per_group)
     frame_sum = jnp.sum(local_vals, axis=(1, 2))
-    totals, squares = (
-        by_axis(group_total(onehot, frame_sum, GROUPS), TILE),
-        by_axis(group_total(onehot, jnp.sum(local_vals * local_vals, axis=(1, 2)), GROUPS), TILE),
+    square_sum = jnp.sum(local_vals * local_vals, axis=(1, 2))
+    totals, squares = tile_total(
+        jnp.stack(
+            [group_total(onehot, frame_sum, GROUPS), group_total(onehot, square_sum, GROUPS)]
+        )
     )
     clip_mean = totals / counts[:, None]
     clip_var = squares / counts[:, None] - clip_mean * clip_mean
@@ -152,11 +182,10 @@
     )
     encoded = lax.all_to_all(encoded_rows[None], TILE, split_axis=1, concat_axis=2, tiled=True)
     spatial_term = contract_rows(columns, grad_block.reshape(-1, channels))
-    pixel_total = lax.axis_size("dp") * frames * height * frame_width
+    pixel_total = lax.axis_size(("row", "core")) * frames * height * frame_width
     grad_scale = 1.0 / math.sqrt(pixel_total)
-    spatial_grad, temporal_grad = lax.psum(
-        (spatial_term * grad_scale, temporal_term * grad_scale), DP_TILE
-    )
+    grads = total_everywhere(jnp.concatenate([spatial_term, temporal_term], axis=0) * grad_scale)
+    spatial_grad, temporal_grad = grads[: 9 * channels], grads[9 * channels :]
     return (
         encoded,
         spatial_grad.reshape(3, 3, channels, channels),
@@ -165,17 +194,17 @@
 
 
 def solution(mesh):
-    finer = Mesh(mesh.devices.reshape(mesh.shape["dp"], 4, 8), ("dp", "tile_0", "tile_1"))
+    finer = Mesh(mesh.devices.reshape(mesh.shape["dp"] // 2, 2, 4, 8), MESH_AXES)
     in_specs = (
-        P("dp", None, TILE, None, None),
-        P("dp", None),
-        P(),
-        P(),
-        P(),
-        P(),
-        P("dp", TILE, None, None, None),
-    )
-    out_specs = (P("dp", TILE, None, None, None), P(), P())
+        P(DP, None, TILE, None, None),
+        P(DP, None),
+        P(),
+        P(),
+        P(),
+        P(),
+        P(DP, TILE, None, None, None),
+    )
+    out_specs = (P(DP, TILE, None, None, None), P(), P())
     return jax.shard_map(
         on_device, mesh=finer, in_specs=in_specs, out_specs=out_specs, check_vma=False
     )

time: 394 us -> 211 us (0.54)
  waiting for transfers between devices: 269 us -> 51.8 us
  blocking collectives: 29 us -> 50 us
  between operations: 14.4 us -> 1.13 us
  starting transfers between devices: 23.5 us -> 35.2 us
  other arithmetic: 19.3 us -> 27.6 us
    psum x1 -> x0, waiting for transfers between devices: 261 us -> none  [on_device(): lax.psum((spatial_term * grad_scale, temporal_term * grad_scale), DP_TILE)]
    all_to_all x0 -> x3, blocking collectives: none -> 50 us  [the longest x2 34.7 us: share_sum(): pieces = lax.all_to_all(pieces, axes, 0, 0, tiled=True)]
    psum x2 -> x0, blocking collectives: 29 us -> none  [by_axis(): return functools.reduce(lax.psum, axes, shard)]
    all_to_all x1, waiting for transfers between devices: 5.61 us -> 22.1 us  [on_device(): lax.all_to_all(encoded_rows[None], TILE, split_axis=1, concat_axis=2, til...]
    all_to_all x0 -> x2, starting transfers between devices: none -> 15.8 us  [the longest x1 11.6 us: tile_total(): return jnp.sum(lax.all_to_all(copies, TILE, 0, 0, tiled=True), axis=0)]
    ppermute x1, waiting for transfers between devices: 0.01 us -> 13.8 us  [extended(): lax.ppermute(tail, axis, [(i, (i + 1) % count) for i in range(ends)])]
    all_to_all x0 -> x2, waiting for transfers between devices: none -> 13.5 us  [the longest x1 7.59 us: tile_total(): return jnp.sum(lax.all_to_all(copies, TILE, 0, 0, tiled=True), axis=0)]
    all_to_all x1, starting transfers between devices: 9.69 us -> 5.57 us  [on_device(): lax.all_to_all(encoded_rows[None], TILE, split_axis=1, concat_axis=2, til...]
  transfers between devices with their start and end apart: 5 -> 8, of which waited for: 4 -> 5; matrix products, arithmetic and copies ran while one was open for 8% -> 11% of each run, Pallas kernels for 0% -> 0%
where the time goes in v1:
time: 211 us; the launch traced here: 208 us
  waiting for transfers between devices  51.8 us (25%)
  blocking collectives  50 us (24%)
  starting transfers between devices  35.2 us (17%)
  other arithmetic  27.6 us (13%)
  matrix products  21.4 us (10%)
  local copies, waits for them, and re-layouts  21 us (10%)
    all_to_all x2, blocking collectives, share_sum(): pieces = lax.all_to_all(pieces, axes, 0, 0, tiled=True)  34.7 us
    all_to_all x1, waiting for transfers between devices, on_device(): lax.all_to_all(encoded_rows[None], TILE, split_axis=1, concat_axis=2, til...  22.1 us
    all_to_all x1, blocking collectives, share_copy(): lax.all_to_all(copies, axes, 0, 0, tiled=True).reshape(-1, piece.shape[-1])  15.3 us
    ppermute x1, waiting for transfers between devices, extended(): lax.ppermute(tail, axis, [(i, (i + 1) % count) for i in range(ends)])  13.8 us
    dot_general x2, matrix products, contract_rows(): lax.dot_general(left, right, (((0,), (0,)), ((), ())), preferred_element_...  12.7 us
    all_to_all x1, starting transfers between devices, tile_total(): return jnp.sum(lax.all_to_all(copies, TILE, 0, 0, tiled=True), axis=0)  11.6 us
    unnamed x48, local copies, waits for them, and re-layouts  11.2 us
    all_to_all x1, waiting for transfers between devices, tile_total(): return jnp.sum(lax.all_to_all(copies, TILE, 0, 0, tiled=True), axis=0)  7.59 us
  transfers between devices with their start and end apart: 8, of which 5 were waited for; matrix products, arithmetic and copies ran while one was open for 11% of the time, Pallas kernels for 0%

profile of v1, /device:TPU:2, one launch (start us, length us, event | category | flops | bytes accessed | tf_op | source)
XLA Modules:
  0.0 208.2 jit_solution(12019660119359863460)
XLA Ops:
  0.7 1.7 convert_reduce_fusion
  2.4 1.6 fusion.15
  4.0 0.8 reduce-window.4
  4.8 0.7 fusion.42
  6.6 0.8 reshape.126
  7.4 11.6 %all-to-all-start = ((f32[32,1,384]{2,1,0:T(1,128)}), f32[32,1,384]{2,1,0:T(1,128)S(1)}, u32[]{:S(2)}, u32[]{:S(2)}) async-start(f32[32,1,384]{2,1,0:T(1,128)} %reshape.126), calls=%async_computation | async-start | bytes 98304 | tf_op jit(solution)/shard_map/all_to_all | solution.py:20
  19.2 1.1 copy.37
  20.2 7.6 %all-to-all-done = f32[32,1,384]{2,1,0:T(1,128)S(1)} async-done(((f32[32,1,384]{2,1,0:T(1,128)}), f32[32,1,384]{2,1,0:T(1,128)S(1)}, u32[]{:S(2)}, u32[]{:S(2)}) %all-to-all-start) | async-done | bytes 49184 | tf_op jit(solution)/shard_map/all_to_all | solution.py:20
  27.8 5.7 %all-to-all-start.2 = ((bf16[1,2,128,8,256]{4,3,1,0,2:T(8,128)(2,1)}), bf16[1,2,128,8,256]{4,3,1,0,2:T(8,128)(2,1)}, u32[]{:S(2)}, u32[]{:S(2)}) async-start(bf16[1,2,128,8,256]{4,3,1,0,2:T(8,128)(2,1)} %copy.37), calls=%async_computation.2 | async-start | bytes 2097152 | tf_op jit(solution)/shard_map/all_to_all | solution.py:175
  34.0 0.8 reduce.3
  36.2 0.7 fusion.24
  37.0 0.8 fusion.50
  37.8 3.4 %collective-permute-start = (bf16[64,1,8,256]{3,2,1,0:T(8,128)(2,1)}, bf16[64,1,8,256]{3,2,1,0:T(8,128)(2,1)}, u32[]{:S(2)}, u32[]{:S(2)}) collective-permute-start(bf16[64,1,8,256]{3,2,1,0:T(8,128)(2,1)} %get-tuple-element.10), channel_id=1, source_target_pairs={{0,1},{1,2},{2,3},{3,4},{4,5},{5,6},{6,7},{7,8},{8,9},{9,10},{10,1... | collective-permute-start | bytes 786440 | tf_op jit(solution)/shard_map/ppermute | solution.py:58
  41.2 4.6 %collective-permute-start.1 = (bf16[64,1,8,256]{3,2,1,0:T(8,128)(2,1)}, bf16[64,1,8,256]{3,2,1,0:T(8,128)(2,1)S(1)}, u32[]{:S(2)}, u32[]{:S(2)}) collective-permute-start(bf16[64,1,8,256]{3,2,1,0:T(8,128)(2,1)} %get-tuple-element.11), channel_id=1, source_target_pairs={{1,0},{2,1},{3,2},{4,3},{5,4},{6,5},{7,6},{8,7},{9,8},{10,9},{11,1... | collective-permute-start | bytes 786440 | tf_op jit(solution)/shard_map/ppermute | solution.py:60
  46.4 1.9 copy.39
  48.3 1.2 broadcast_compare_fusion.2
  49.6 13.8 %collective-permute-done = bf16[64,1,8,256]{3,2,1,0:T(8,128)(2,1)} collective-permute-done((bf16[64,1,8,256]{3,2,1,0:T(8,128)(2,1)}, bf16[64,1,8,256]{3,2,1,0:T(8,128)(2,1)}, u32[]{:S(2)}, u32[]{:S(2)}) %collective-permute-start) | collective-permute-done | bytes 262176 | tf_op jit(solution)/shard_map/ppermute | solution.py:58
  63.4 2.5 %fusion.5 = bf16[64,6,10,256]{3,2,1,0:T(8,128)(2,1)S(1)} fusion(bf16[64,1,8,256]{3,2,1,0:T(8,128)(2,1)S(1)} %collective-permute-done.1, bf16[64,4,8,256]{3,2,1,0:T(8,128)(2,1)S(1)} %fusion.24, bf16[64,1,8,256]{3,2,1,0:T(8,128)(2,1)} %collective-permute-done), kind=kLoop, calls=%fused_computation.8 | loop fusion | flops 11796480 | bytes 3538944 | tf_op jit(solution)/shard_map/concatenate | solution.py:56
  66.0 1.1 fusion.31
  67.5 0.8 constant_dynamic-update-slice_fusion
  69.1 3.6 %copy-done.11 = bf16[64,4,8,2304]{3,2,1,0:T(8,128)(2,1)} copy-done((bf16[64,4,8,2304]{3,2,1,0:T(8,128)(2,1)}, bf16[64,4,8,2304]{3,2,1,0:T(8,128)(2,1)S(1)}, u32[]{:S(2)}) %copy-start.11) | copy-done | bytes 9437208
  72.8 3.7 %fusion.25 = bf16[64,4,8,256]{3,2,1,0:T(8,128)(2,1)} fusion(bf16[1,64,4,8,256]{4,3,2,1,0:T(8,128)(2,1)S(1)} %copy-done.1, bf16[64,4,8,2304]{3,2,1,0:T(8,128)(2,1)S(1)} %slice_dynamic-update-slice_fusion, bf16[2304,256,1,1]{1,0,3,2:T(8,128)(2,1)S(1)} %bitcast.135), kind=kOutput, calls=%fused_computation.32 | convolution fusion | flops 2417491968 | bytes 12713984 | tf_op jit(solution)/shard_map/dot_general | solution.py:171
  76.5 1.3 copy.38
  77.8 3.3 %broadcast_select_fusion.1 = (bf16[64,4,8,256]{3,2,1,0:T(8,128)(2,1)S(1)}, bf16[64,4,8,256]{3,2,1,0:T(8,128)(2,1)S(1)}, bf16[64,4,8,256]{3,2,1,0:T(8,128)(2,1)S(1)}, bf16[64,4,8,256]{3,2,1,0:T(8,128)(2,1)}) fusion(bf16[64,4,8,256]{3,2,1,0:T(8,128)(2,1)} %fusion.25, pred[64]{0:T(512)(128)(4,1)S(1)} %get-tuple-element.19, pred[64]{0:T(512)(128)(4,1)S(1)} %copy-done.14, ...), kind=kLoop, calls=%fused_computation.57 | loop fusion | flops 2097152 | bytes 6291648 | tf_op jit(solution)/shard_map/jit(_where)/select_n | solution.py:103
  82.5 1.9 fusion.52
  84.4 1.6 slice_select_fusion.1
  85.9 10.8 %convolution_bitcast_fusion = f32[2304,256]{1,0:T(8,128)} fusion(bf16[64,4,8,2304]{3,2,1,0:T(8,128)(2,1)} %copy-done.11, bf16[64,4,8,256]{3,2,1,0:T(8,128)(2,1)S(1)} %bitcast.140, bf16[768,256,1,1]{1,0,3,2:T(8,128)(2,1)} %bitcast.150, bf16[64,4,8,256]{3,2,1,0:T(8,128)(2,1)} %get-tuple-element.6, bf16[64,4,8,256]{3,2,1,0:T(8,128)(2,1)} %get-tuple-element.5, ...), kind=kOutput, calls=%fused_computation.3 | convolution fusion | flops 3232235520 | bytes 16384000 | tf_op jit(solution)/shard_map/dot_general | solution.py:118
  96.8 2.2 %maximum_multiply_fusion = f32[3072,256]{1,0:T(8,128)S(1)} fusion(f32[768,256]{1,0:T(8,128)} %fusion.52, f32[2304,256]{1,0:T(8,128)} %convolution_bitcast_fusion), kind=kLoop, calls=%fused_computation.16 | loop fusion | flops 1572864 | bytes 6291456 | tf_op jit(solution)/shard_map/mul | solution.py:187
  99.0 1.6 copy-done.2
  100.8 2.4 %collective-permute-done.2 = bf16[1536,256]{1,0:T(8,128)(2,1)} collective-permute-done((bf16[1536,256]{1,0:T(8,128)(2,1)S(1)}, bf16[1536,256]{1,0:T(8,128)(2,1)}, u32[]{:S(2)}, u32[]{:S(2)}) %collective-permute-start.2) | collective-permute-done | bytes 786464 | tf_op jit(solution)/shard_map/ppermute | solution.py:41
  103.2 1.8 fusion.26
  105.0 17.0 %all_to_all.58 = bf16[4,384,256]{2,1,0:T(8,128)(2,1)} all-to-all(bf16[4,384,256]{2,1,0:T(8,128)(2,1)S(1)} %bitcast.143), channel_id=1, replica_groups=mesh['row'=4,'core'=2,'tile_0'=4,'tile_1'=8] {'row'}, dimensions={0} | all-to-all | bytes 1572864 | tf_op jit(solution)/shard_map/all_to_all | solution.py:26
  122.0 2.1 reduce_sum.84
  124.0 1.0 reshape.117
  125.0 17.7 %all_to_all.59 = bf16[32,12,256]{2,1,0:T(8,128)(2,1)} all-to-all(bf16[32,12,256]{2,1,0:T(8,128)(2,1)S(1)} %reshape.117), channel_id=1, replica_groups=mesh['row'=4,'core'=2,'tile_0'=4,'tile_1'=8] {'tile_0','tile_1'}, dimensions={0} | all-to-all | bytes 393216 | tf_op jit(solution)/shard_map/all_to_all | solution.py:26
  142.7 1.0 reduce_sum.85
  143.8 15.3 %all_to_all.60 = bf16[32,12,256]{2,1,0:T(8,128)(2,1)S(1)} all-to-all(bf16[32,12,256]{2,1,0:T(8,128)(2,1)S(1)} %broadcast_in_dim.97), channel_id=1, replica_groups=mesh['row'=4,'core'=2,'tile_0'=4,'tile_1'=8] {'tile_0','tile_1'}, dimensions={0} | all-to-all | bytes 393216 | tf_op jit(solution)/shard_map/all_to_all | solution.py:32
  159.1 0.7 broadcast_in_dim.98
  159.8 1.9 broadcast_in_dim.99
  161.7 4.2 %all-to-all-start.6 = ((bf16[4,384,256]{2,1,0:T(8,128)(2,1)}), bf16[4,384,256]{2,1,0:T(8,128)(2,1)}, u32[]{:S(2)}, u32[]{:S(2)}) async-start(bf16[4,384,256]{2,1,0:T(8,128)(2,1)} %broadcast_in_dim.99), calls=%async_computation.6 | async-start | bytes 1572864 | tf_op jit(solution)/shard_map/all_to_all | solution.py:32
  165.9 3.6 %fusion.29 = bf16[1,64,4,8,256]{4,3,2,0,1:T(8,128)(2,1)} fusion(bf16[768,256,1,1]{1,0,3,2:T(8,128)(2,1)} %bitcast.149, bf16[64,4,8,256]{3,2,1,0:T(8,128)(2,1)} %fusion.25, bf16[64,4,8,256]{3,2,1,0:T(8,128)(2,1)S(1)} %copy-done.4, bf16[64,4,8,256]{3,2,1,0:T(8,128)(2,1)} %copy-done.5, bf16[64,4,8,256]{3,2,1,0:T(8,128)(2,1)S(1)} %get-tuple-element.7), kind=kOutput, calls=%fused_computation.39 | convolution fusion | flops 816316416 | bytes 5636096 | tf_op jit(solution)/shard_map/dot_general | solution.py:128
  169.5 5.9 %all-to-all-done.6 = bf16[4,384,256]{2,1,0:T(8,128)(2,1)} async-done(((bf16[4,384,256]{2,1,0:T(8,128)(2,1)}), bf16[4,384,256]{2,1,0:T(8,128)(2,1)}, u32[]{:S(2)}, u32[]{:S(2)}) %all-to-all-start.6) | async-done | bytes 786464 | tf_op jit(solution)/shard_map/all_to_all | solution.py:32
  175.4 5.6 %all-to-all-start.1 = ((bf16[1,64,4,8,256]{4,3,2,0,1:T(8,128)(2,1)}), bf16[1,64,4,8,256]{4,3,2,0,1:T(8,128)(2,1)S(1)}, u32[]{:S(2)}, u32[]{:S(2)}) async-start(bf16[1,64,4,8,256]{4,3,2,0,1:T(8,128)(2,1)} %fusion.29), calls=%async_computation.1 | async-start | bytes 2097152 | tf_op jit(solution)/shard_map/all_to_all | solution.py:183
  181.1 22.1 %all-to-all-done.1 = bf16[1,64,4,8,256]{4,3,2,0,1:T(8,128)(2,1)S(1)} async-done(((bf16[1,64,4,8,256]{4,3,2,0,1:T(8,128)(2,1)}), bf16[1,64,4,8,256]{4,3,2,0,1:T(8,128)(2,1)S(1)}, u32[]{:S(2)}, u32[]{:S(2)}) %all-to-all-start.1) | async-done | bytes 1048608 | tf_op jit(solution)/shard_map/all_to_all | solution.py:183
  203.2 1.1 copy.36
  204.3 1.2 broadcast_select_fusion.3
  205.5 0.9 maximum_convert_fusion.1
  206.7 1.6 slice.86
  (75 shorter events, 6.9 us)
Async XLA Ops:
  0.6 68.5 %copy-start = (bf16[3,3,256,256]{3,2,1,0:T(8,128)(2,1)S(1)}, bf16[3,3,256,256]{3,2,1,0:T(8,128)(2,1)}, u32[]{:S(2)}) copy-start(bf16[3,3,256,256]{3,2,1,0:T(8,128)(2,1)} %param.11) | copy-start | bytes 3538948
  0.6 18.4 %copy-start.18 = (s32[1,6]{1,0:T(1,128)S(1)}, s32[1,6]{1,0:T(1,128)}, u32[]{:S(2)}) copy-start(s32[1,6]{1,0:T(1,128)} %param.8) | copy-start | bytes 76
  0.7 18.5 %copy-start.6 = (bf16[1,2,128,8,256]{4,3,2,1,0:T(8,128)(2,1)S(1)}, bf16[1,2,128,8,256]{4,3,2,1,0:T(8,128)(2,1)}, u32[]{:S(2)}) copy-start(bf16[1,2,128,8,256]{4,3,2,1,0:T(8,128)(2,1)} %param.13) | copy-start | bytes 3145732
  5.9 30.3 %copy-start.1 = (bf16[1,64,4,8,256]{4,3,2,1,0:T(8,128)(2,1)S(1)}, bf16[1,64,4,8,256]{4,3,2,1,0:T(8,128)(2,1)}, u32[]{:S(2)}) copy-start(bf16[1,64,4,8,256]{4,3,2,1,0:T(8,128)(2,1)} %param.7) | copy-start | bytes 3145732
  6.0 30.2 %copy-start.12 = (f32[256]{0:T(256)S(1)}, f32[256]{0:T(256)}, u32[]{:S(2)}) copy-start(f32[256]{0:T(256)} %param.10) | copy-start | bytes 3076
  6.0 30.2 %copy-start.13 = (f32[256]{0:T(256)S(1)}, f32[256]{0:T(256)}, u32[]{:S(2)}) copy-start(f32[256]{0:T(256)} %param.9) | copy-start | bytes 3076
  7.4 20.4 %all-to-all-start = ((f32[32,1,384]{2,1,0:T(1,128)}), f32[32,1,384]{2,1,0:T(1,128)S(1)}, u32[]{:S(2)}, u32[]{:S(2)}) async-start(f32[32,1,384]{2,1,0:T(1,128)} %reshape.126), calls=%async_computation | async-start | bytes 98304 | tf_op jit(solution)/shard_map/all_to_all | solution.py:20
  19.1 17.8 %copy-start.17 = (s32[64]{0:T(128)}, s32[64]{0:T(128)S(1)}, u32[]{:S(2)}) copy-start(s32[64]{0:T(128)S(1)} %select_reduce_fusion) | copy-start | bytes 772
  27.8 48.7 %all-to-all-start.2 = ((bf16[1,2,128,8,256]{4,3,1,0,2:T(8,128)(2,1)}), bf16[1,2,128,8,256]{4,3,1,0,2:T(8,128)(2,1)}, u32[]{:S(2)}, u32[]{:S(2)}) async-start(bf16[1,2,128,8,256]{4,3,1,0,2:T(8,128)(2,1)} %copy.37), calls=%async_computation.2 | async-start | bytes 2097152 | tf_op jit(solution)/shard_map/all_to_all | solution.py:175
  35.7 5.5 %copy-start.7 = (f32[64,256]{1,0:T(8,128)}, f32[64,256]{1,0:T(8,128)S(1)}, u32[]{:S(2)}) copy-start(f32[64,256]{1,0:T(8,128)S(1)} %fusion.47) | copy-start | bytes 196612
  36.2 5.0 %copy-start.9 = (f32[64,256]{1,0:T(8,128)}, f32[64,256]{1,0:T(8,128)S(1)}, u32[]{:S(2)}) copy-start(f32[64,256]{1,0:T(8,128)S(1)} %fusion.45) | copy-start | bytes 196612
  37.8 25.6 %collective-permute-start = (bf16[64,1,8,256]{3,2,1,0:T(8,128)(2,1)}, bf16[64,1,8,256]{3,2,1,0:T(8,128)(2,1)}, u32[]{:S(2)}, u32[]{:S(2)}) collective-permute-start(bf16[64,1,8,256]{3,2,1,0:T(8,128)(2,1)} %get-tuple-element.10), channel_id=1, source_target_pairs={{0,1},{1,2},{2,3},{3,4},{4,5},{5,6},{6,7},{7,8},{8,9},{9,10},{10,1... | collective-permute-start | bytes 786440 | tf_op jit(solution)/shard_map/ppermute | solution.py:58
  41.2 22.2 %collective-permute-start.1 = (bf16[64,1,8,256]{3,2,1,0:T(8,128)(2,1)}, bf16[64,1,8,256]{3,2,1,0:T(8,128)(2,1)S(1)}, u32[]{:S(2)}, u32[]{:S(2)}) collective-permute-start(bf16[64,1,8,256]{3,2,1,0:T(8,128)(2,1)} %get-tuple-element.11), channel_id=1, source_target_pairs={{1,0},{2,1},{3,2},{4,3},{5,4},{6,5},{7,6},{8,7},{9,8},{10,9},{11,1... | collective-permute-start | bytes 786440 | tf_op jit(solution)/shard_map/ppermute | solution.py:60
  65.9 1.5 copy-start.8
  66.0 1.5 copy-start.10
  69.1 3.6 %copy-start.11 = (bf16[64,4,8,2304]{3,2,1,0:T(8,128)(2,1)}, bf16[64,4,8,2304]{3,2,1,0:T(8,128)(2,1)S(1)}, u32[]{:S(2)}) copy-start(bf16[64,4,8,2304]{3,2,1,0:T(8,128)(2,1)S(1)} %slice_dynamic-update-slice_fusion) | copy-start | bytes 28311556
  72.8 5.1 %copy-start.14 = (pred[64]{0:T(512)(128)(4,1)S(1)}, pred[64]{0:T(512)(128)(4,1)}, u32[]{:S(2)}) copy-start(pred[64]{0:T(512)(128)(4,1)} %get-tuple-element.21) | copy-start | bytes 196
  81.1 1.0 copy-start.3
  81.1 1.3 copy-start.5
  82.5 1.9 copy-start.15
  82.5 1.9 copy-start.16
  98.9 1.6 copy-start.2
  100.7 2.5 %collective-permute-start.2 = (bf16[1536,256]{1,0:T(8,128)(2,1)S(1)}, bf16[1536,256]{1,0:T(8,128)(2,1)}, u32[]{:S(2)}, u32[]{:S(2)}) collective-permute-start(bf16[1536,256]{1,0:T(8,128)(2,1)S(1)} %fusion.32), channel_id=1, source_target_pairs={{0,32},{32,0},{1,33},{33,1},{2,34},{34,2},{3,35},{35,3},{4,36},{36... | collective-permute-start | bytes 2359304 | tf_op jit(solution)/shard_map/ppermute | solution.py:41
  122.0 43.9 %copy-start.4 = (bf16[64,4,8,256]{3,2,1,0:T(8,128)(2,1)S(1)}, bf16[64,4,8,256]{3,2,1,0:T(8,128)(2,1)}, u32[]{:S(2)}) copy-start(bf16[64,4,8,256]{3,2,1,0:T(8,128)(2,1)} %copy-done.3) | copy-start | bytes 3145732
  161.7 13.7 %all-to-all-start.6 = ((bf16[4,384,256]{2,1,0:T(8,128)(2,1)}), bf16[4,384,256]{2,1,0:T(8,128)(2,1)}, u32[]{:S(2)}, u32[]{:S(2)}) async-start(bf16[4,384,256]{2,1,0:T(8,128)(2,1)} %broadcast_in_dim.99), calls=%async_computation.6 | async-start | bytes 1572864 | tf_op jit(solution)/shard_map/all_to_all | solution.py:32
  175.4 27.8 %all-to-all-start.1 = ((bf16[1,64,4,8,256]{4,3,2,0,1:T(8,128)(2,1)}), bf16[1,64,4,8,256]{4,3,2,0,1:T(8,128)(2,1)S(1)}, u32[]{:S(2)}, u32[]{:S(2)}) async-start(bf16[1,64,4,8,256]{4,3,2,0,1:T(8,128)(2,1)} %fusion.29), calls=%async_computation.1 | async-start | bytes 2097152 | tf_op jit(solution)/shard_map/all_to_all | solution.py:183
  181.0 23.3 %collective-permute-start.3 = (bf16[1536,256]{1,0:T(8,128)(2,1)}, bf16[1536,256]{1,0:T(8,128)(2,1)S(1)}, u32[]{:S(2)}, u32[]{:S(2)}) collective-permute-start(bf16[1536,256]{1,0:T(8,128)(2,1)} %bitcast.39), channel_id=1, source_target_pairs={{0,32},{32,0},{1,33},{33,1},{2,34},{34,2},{3,35},{35,3},{4,36},{36... | collective-permute-start | bytes 2359304 | tf_op jit(solution)/shard_map/ppermute | solution.py:44

commit v2 on v0

v2 whole, which is shorter than its diff:
```python
import functools
import math

import jax
import jax.numpy as jnp
from jax import lax
from jax.experimental import pallas as pl
from jax.experimental.pallas import tpu as pltpu
from jax.sharding import Mesh
from jax.sharding import PartitionSpec as P


GROUPS = 32
LANES = 128
SLOTS = 8
TILE = ("tile_0", "tile_1")
DP = ("row", "core")
PLANE = ("row", "tile_0")
MESH_AXES = ("row", "core", "tile_0", "tile_1")
SWAP = [(0, 1), (1, 0)]

norm_eps = 1e-05

VMEM = pl.BlockSpec(memory_space=pltpu.VMEM)
SMEM = pl.BlockSpec(memory_space=pltpu.SMEM)
HBM = pl.BlockSpec(memory_space=pltpu.HBM)
exact_dot = functools.partial(
    jnp.dot, precision=lax.Precision.HIGHEST, preferred_element_type=jnp.float32
)
dot = functools.partial(jnp.dot, preferred_element_type=jnp.float32)


def clip_starts(lengths_ref):
    starts = [jnp.int32(0)]
    for clip in range(lengths_ref.shape[1] - 1):
        starts.append(starts[-1] + lengths_ref[0, clip])
    return starts


def clip_of(starts, frame):
    clip = jnp.int32(0)
    first = jnp.int32(0)
    for number, start in enumerate(starts[1:], 1):
        inside = frame >= start
        clip = jnp.where(inside, number, clip)
        first = jnp.where(inside, start, first)
    return clip, first


def reach(starts, frame, steps, total):
    _, first = clip_of(starts, frame + steps)
    keep = (frame + steps < total) & (frame >= first)
    return jnp.where(keep, jnp.float32(1.0), jnp.float32(0.0))


def picker(rows, columns, offset, per_group, flip):
    row = lax.broadcasted_iota(jnp.int32, (rows, columns), 0)
    column = lax.broadcasted_iota(jnp.int32, (rows, columns), 1)
    lane, channel = (row, column) if flip else (column, row)
    return (lane == channel // per_group + offset).astype(jnp.float32)


def stats_kernel(lengths_ref, video_ref, out_ref, top_ref, bottom_ref, sum_ref, square_ref):
    frames, rows, _, channels = video_ref.shape
    starts = clip_starts(lengths_ref)
    top_ref[...] = video_ref[:, 0]
    bottom_ref[...] = video_ref[:, rows - 1]
    sum_ref[...] = jnp.zeros_like(sum_ref)
    square_ref[...] = jnp.zeros_like(square_ref)

    def step(frame, carry):
        clip, _ = clip_of(starts, frame)
        cells = video_ref[frame].astype(jnp.float32)
        sum_ref[clip] += jnp.sum(cells, axis=0)
        square_ref[clip] += jnp.sum(cells * cells, axis=0)
        return carry

    lax.fori_loop(0, frames, step, 0, unroll=4)
    per_group = channels // GROUPS
    sums = jnp.sum(sum_ref[...], axis=1)
    squares = jnp.sum(square_ref[...], axis=1)
    total = exact_dot(sums, picker(channels, LANES, 0, per_group, False)) + exact_dot(
        squares, picker(channels, LANES, GROUPS, per_group, False)
    )
    out_ref[...] = jnp.broadcast_to(total[None], out_ref.shape)


def backward_kernel(
    grad_scale,
    lengths_ref,
    place_ref,
    cot_ref,
    weight_ref,
    kept_ref,
    block_ref,
    send_ref,
    keep_ref,
    active_ref,
    later_ref,
    grad_ref,
    wide_ref,
    part_ref,
    sem,
):
    load = pltpu.make_async_copy(kept_ref, active_ref, sem)
    load.start()
    frames, rows, width, channels = cot_ref.shape
    starts = clip_starts(lengths_ref)

    def step(pair, carry):
        for steps in range(3):
            parts = []
            for half in range(2):
                frame = pair * 2 + half
                source = jnp.minimum(frame + steps, frames - 1)
                cells = cot_ref[source].astype(jnp.float32)
                if steps:
                    cells = cells * reach(starts, frame, steps, frames)
                parts.append(cells)
            both = jnp.concatenate(parts, axis=1).astype(jnp.bfloat16)
            at = pl.ds(pl.multiple_of(pair * 2 * width, 2 * width), 2 * width)
            later_ref[:, at, steps * channels : (steps + 1) * channels] = both
        return carry

    lax.fori_loop(0, frames // 2, step, 0, unroll=2)
    for k in range(3):
        wide_ref[k * channels : (k + 1) * channels, :] = (
            weight_ref[k].astype(jnp.float32).T.astype(jnp.bfloat16)
        )
    for row in range(rows):
        pulled = dot(later_ref[row], wide_ref[...])
        grad_ref[row] = (later_ref[row, :, :channels].astype(jnp.float32) + pulled).astype(
            jnp.bfloat16
        )
    cells = frames * width
    grads = grad_ref[...].reshape(rows * cells, channels)
    flip = functools.partial(
        lax.dot_general,
        dimension_numbers=(((0,), (0,)), ((), ())),
        preferred_element_type=jnp.float32,
    )
    load.wait()
    span = 3 * channels
    for i in range(3):
        tap = flip(active_ref[i : i + rows].reshape(rows * cells, span), grads) * grad_scale
        part_ref[i // 2, (i % 2) * span : (i % 2 + 1) * span, :] = tap
    later = later_ref[...].reshape(rows * cells, span)
    temporal = flip(block_ref[...].reshape(rows * cells, channels), later) * grad_scale
    for k in range(3):
        part_ref[1, span + k * channels : span + (k + 1) * channels, :] = temporal[
            :, k * channels : (k + 1) * channels
        ]
    core = place_ref[0, 2]
    send_ref[...] = part_ref[1 - core].astype(jnp.bfloat16)
    keep_ref[...] = part_ref[core]


def column_shift(cells, step):
    column = lax.broadcasted_iota(jnp.int32, cells.shape, 1)
    width = cells.shape[1]
    edge = 0 if step == 1 else width - 1
    return jnp.where(column == edge, 0.0, pltpu.roll(cells, step % width, 1))


def forward_kernel(
    height,
    lengths_ref,
    place_ref,
    total_ref,
    video_ref,
    above_ref,
    below_ref,
    spatial_ref,
    temporal_ref,
    gain_ref,
    bias_ref,
    encoded_ref,
    kept_ref,
    block_ref,
    mean_ref,
    scale_ref,
    active_ref,
    lift_ref,
    now_ref,
    total_in,
    above_in,
    below_in,
    sems,
):
    frames, rows, width, channels = video_ref.shape
    per_group = channels // GROUPS
    cells_in = frames * width
    starts = clip_starts(lengths_ref)
    loads = [
        pltpu.make_async_copy(source, target, sems.at[number])
        for number, (source, target) in enumerate(
            ((total_ref, total_in), (above_ref, above_in), (below_ref, below_in))
        )
    ]
    for load in loads:
        load.start()

    loads[0].wait()
    total = jnp.sum(total_in[...], axis=0)
    sums = exact_dot(total, picker(LANES, channels, 0, per_group, True))
    squares = exact_dot(total, picker(LANES, channels, GROUPS, per_group, True))
    slot = lax.broadcasted_iota(jnp.int32, sums.shape, 0)
    counts = jnp.ones_like(sums)
    for clip in range(lengths_ref.shape[1]):
        cells = lengths_ref[0, clip].astype(jnp.float32) * (height * width * per_group)
        counts = jnp.where(slot == clip, cells, counts)
    mean = sums / counts
    var = jnp.maximum(squares / counts - mean * mean, 0.0)
    mean_ref[...] = mean
    scale_ref[...] = lax.rsqrt(var + norm_eps) * gain_ref[...]

    bias = bias_ref[...][None]
    has_above = place_ref[0, 0].astype(jnp.float32)
    has_below = place_ref[0, 1].astype(jnp.float32)

    loads[1].wait()
    loads[2].wait()

    def normalise(pair, carry):
        shifted = [[], [], []]
        for half in range(2):
            frame = pair * 2 + half
            clip, _ = clip_of(starts, frame)
            mean_row = mean_ref[pl.ds(clip, 1), :][None]
            scale_row = scale_ref[pl.ds(clip, 1), :][None]

            def activate(cells):
                normed = (cells.astype(jnp.float32) - mean_row) * scale_row + bias
                return normed / (1.0 + jnp.exp(-normed))

            active = jnp.concatenate(
                [
                    activate(above_in[frame][None]) * has_above,
                    activate(video_ref[frame]),
                    activate(below_in[frame][None]) * has_below,
                ],
                axis=0,
            )
            active = active.astype(jnp.bfloat16).astype(jnp.float32)
            shifted[0].append(column_shift(active, 1))
            shifted[1].append(active)
            shifted[2].append(column_shift(active, -1))
        at = pl.ds(pl.multiple_of(pair * 2 * width, 2 * width), 2 * width)
        for j in range(3):
            active_ref[:, at, j * channels : (j + 1) * channels] = jnp.concatenate(
                shifted[j], axis=1
            ).astype(jnp.bfloat16)
        return carry

    lax.fori_loop(0, frames // 2, normalise, 0)
    save = pltpu.make_async_copy(active_ref, kept_ref, sems.at[3])
    save.start()

    lift_ref[:, : 2 * width, :] = jnp.zeros((2, 2 * width, channels), jnp.float32)
    for row in range(rows):
        conv = dot(active_ref[row], spatial_ref[0])
        conv += dot(active_ref[row + 1], spatial_ref[1])
        conv += dot(active_ref[row + 2], spatial_ref[2])
        video_row = video_ref[:, row].astype(jnp.float32).reshape(cells_in, channels)
        block = (video_row + conv).astype(jnp.bfloat16)
        block_ref[row] = block
        now = block.astype(jnp.float32) + dot(block, temporal_ref[0])
        now_ref[...] = now
        lift_ref[0, 2 * width :, :] = dot(block, temporal_ref[1])
        lift_ref[1, 2 * width :, :] = dot(block, temporal_ref[2])

        def earlier(frame, carry):
            _, first = clip_of(starts, frame)
            at = frame * width
            out = now_ref[pl.ds(at, width), :]
            for k in (1, 2):
                keep = jnp.where(frame - first >= k, jnp.float32(1.0), jnp.float32(0.0))
                out += keep * lift_ref[k - 1, pl.ds(at + (2 - k) * width, width), :]
            encoded_ref[frame, row] = out.astype(jnp.bfloat16)
            return carry

        lax.fori_loop(0, frames, earlier, 0, unroll=4)

    save.wait()


def finish_kernel(place_ref, whole_ref, facing_ref, spatial_ref, temporal_ref):
    held = spatial_ref.shape[0]
    pieces = 16
    size = whole_ref.shape[0] // pieces
    turn, upper = (0, 1, 1, 0), (0, 0, 1, 1)

    def fill(side, source_ref):
        one, two = (turn, upper) if side == 0 else (upper, turn)
        for number in range(pieces):
            a, b = divmod(number, 4)
            spot = one[a] * 8 + two[a] * 4 + one[b] * 2 + two[b]
            at = (side * pieces + spot) * size
            piece = source_ref[number * size : (number + 1) * size, :].astype(jnp.float32)
            if at < held:
                spatial_ref[at : at + size, :] = piece
            else:
                temporal_ref[at - held : at - held + size, :] = piece

    @pl.when(place_ref[0, 2] == 0)
    def _():
        fill(0, whole_ref)
        fill(1, facing_ref)

    @pl.when(place_ref[0, 2] != 0)
    def _():
        fill(1, whole_ref)
        fill(0, facing_ref)


def share(pieces, axes):
    return lax.all_to_all(pieces, axes, 0, 0, tiled=True)


def copies(piece, axes):
    return jnp.broadcast_to(piece[None], (lax.axis_size(axes),) + piece.shape)


def summed(pieces):
    return jnp.sum(pieces.astype(jnp.float32), axis=0).astype(jnp.bfloat16)


def on_device(
    video_in, clip_lengths, norm_gain, norm_bias, spatial_weight, temporal_weight, cotangent
):
    tile_count = lax.axis_size(TILE)
    tile_index = lax.axis_index(TILE)
    video = video_in[0]
    frames, strip_rows, width, channels = video.shape
    height = strip_rows * tile_count
    span = 3 * channels
    cells = frames * width
    params = functools.partial(pltpu.CompilerParams, vmem_limit_bytes=24 * 1024 * 1024)
    f32, bf16 = jnp.float32, jnp.bfloat16

    edge = jax.ShapeDtypeStruct((frames, width, channels), bf16)
    part, top, bottom = pl.pallas_call(
        stats_kernel,
        out_shape=(jax.ShapeDtypeStruct((tile_count, SLOTS, LANES), f32), edge, edge),
        in_specs=[SMEM, VMEM],
        out_specs=(VMEM, VMEM, VMEM),
        scratch_shapes=[pltpu.VMEM((SLOTS, width, channels), f32)] * 2,
        compiler_params=params(),
        name="stats",
    )(clip_lengths, video)
    ends = tile_count - 1
    above = lax.ppermute(bottom, TILE, [(i, i + 1) for i in range(ends)])
    below = lax.ppermute(top, TILE, [(i + 1, i) for i in range(ends)])
    totals = share(part, TILE)

    held = frames // tile_count
    by_rows = cotangent[0].reshape(held, tile_count, strip_rows, width, channels)
    by_rows = jnp.transpose(by_rows, (1, 0, 2, 3, 4))
    cot_rows = share(by_rows, TILE)
    cot_rows = cot_rows.reshape(frames, strip_rows, width, channels)

    place = jnp.stack(
        [tile_index > 0, tile_index < tile_count - 1, lax.axis_index("core") > 0]
    ).astype(jnp.int32)[None]

    encoded_rows, active, block = pl.pallas_call(
        functools.partial(forward_kernel, height),
        out_shape=(
            jax.ShapeDtypeStruct((frames, strip_rows, width, channels), bf16),
            jax.ShapeDtypeStruct((strip_rows + 2, cells, span), bf16),
            jax.ShapeDtypeStruct((strip_rows, cells, channels), bf16),
        ),
        in_specs=[SMEM, SMEM, HBM, VMEM, HBM, HBM] + [VMEM] * 4,
        out_specs=(VMEM, HBM, VMEM),
        scratch_shapes=[
            pltpu.VMEM((SLOTS, channels), f32),
            pltpu.VMEM((SLOTS, channels), f32),
            pltpu.VMEM((strip_rows + 2, cells, span), bf16),
            pltpu.VMEM((2, cells + 2 * width, channels), f32),
            pltpu.VMEM((cells, channels), f32),
            pltpu.VMEM(totals.shape, f32),
            pltpu.VMEM(above.shape, bf16),
            pltpu.VMEM(below.shape, bf16),
            pltpu.SemaphoreType.DMA((4,)),
        ],
        compiler_params=params(vmem_limit_bytes=60 << 20),
        name="forward",
    )(
        clip_lengths,
        place,
        totals,
        video,
        above,
        below,
        spatial_weight.reshape(3, span, channels),
        temporal_weight,
        norm_gain[None],
        norm_bias[None],
    )
    encoded = share(
        encoded_rows.reshape(tile_count, held, strip_rows, width, channels), TILE
    )
    encoded = jnp.transpose(encoded, (1, 0, 2, 3, 4)).reshape(cotangent.shape)

    pixel_total = lax.axis_size(DP) * frames * height * width
    half_rows = 2 * span
    send, keep = pl.pallas_call(
        functools.partial(backward_kernel, 1.0 / math.sqrt(pixel_total)),
        out_shape=(
            jax.ShapeDtypeStruct((half_rows, channels), bf16),
            jax.ShapeDtypeStruct((half_rows, channels), f32),
        ),
        in_specs=[SMEM, SMEM, VMEM, VMEM, HBM, VMEM],
        out_specs=(VMEM, VMEM),
        scratch_shapes=[
            pltpu.VMEM(active.shape, bf16),
            pltpu.VMEM((strip_rows, cells, span), bf16),
            pltpu.VMEM((strip_rows, cells, channels), bf16),
            pltpu.VMEM((span, channels), bf16),
            pltpu.VMEM((2, half_rows, channels), f32),
            pltpu.SemaphoreType.DMA,
        ],
        compiler_params=params(vmem_limit_bytes=60 << 20),
        name="backward",
    )(clip_lengths, place, cot_rows, temporal_weight, active, block)

    core = lax.axis_index("core")
    mine = keep + lax.ppermute(send, "core", SWAP).astype(f32)
    even = [(0, 1), (1, 0), (2, 3), (3, 2)]
    odd = [(1, 2), (2, 1), (3, 0), (0, 3)]
    for axis in ("row", "tile_0"):
        spot = lax.axis_index(axis)
        turn = jnp.where((spot == 1) | (spot == 2), 1, 0)
        upper = jnp.where(spot >= 2, 1, 0)
        for step in range(2):
            side = jnp.where(core == step, turn, upper)
            one, two = (even, odd) if step == 0 else (odd, even)
            if axis == "row":
                axes = ("row", "core")
                pairs = [(2 * a, 2 * b) for a, b in one] + [(2 * a + 1, 2 * b + 1) for a, b in two]
            else:
                axes = ("core", "tile_0")
                pairs = one + [(a + 4, b + 4) for a, b in two]
            sides = mine.reshape(2, -1, channels)
            away = lax.dynamic_index_in_dim(sides, 1 - side, 0, keepdims=False).astype(bf16)
            stay = lax.dynamic_index_in_dim(sides, side, 0, keepdims=False)
            mine = stay + lax.ppermute(away, axes, pairs).astype(f32)
    pieces = share(copies(mine.astype(bf16), "tile_1"), "tile_1")
    piece = summed(pieces)
    whole = share(copies(piece, PLANE), PLANE).reshape(half_rows, channels)
    facing = lax.ppermute(whole, "core", SWAP)
    spatial_grad, temporal_grad = pl.pallas_call(
        finish_kernel,
        out_shape=(
            jax.ShapeDtypeStruct((3 * span, channels), f32),
            jax.ShapeDtypeStruct((span, channels), f32),
        ),
        in_specs=[SMEM, VMEM, VMEM],
        out_specs=(VMEM, VMEM),
        compiler_params=params(),
        name="finish",
    )(place, whole, facing)
    return (
        encoded,
        spatial_grad.reshape(3, 3, channels, channels),
        temporal_grad.reshape(3, channels, channels),
    )


def solution(mesh):
    finer = Mesh(mesh.devices.reshape(mesh.shape["dp"] // 2, 2, 4, 8), MESH_AXES)
    in_specs = (
        P(DP, None, TILE, None, None),
        P(DP, None),
        P(),
        P(),
        P(),
        P(),
        P(DP, TILE, None, None, None),
    )
    out_specs = (P(DP, TILE, None, None, None), P(), P())
    return jax.shard_map(
        on_device, mesh=finer, in_specs=in_specs, out_specs=out_specs, check_vma=False
    )
```

time: 394 us -> 181 us (0.46)
  waiting for transfers between devices: 269 us -> 68.3 us
  Pallas kernels: 0 us -> 29 us
  matrix products: 19.8 us -> 0 us
  other arithmetic: 19.3 us -> 2.32 us
  between operations: 14.4 us -> 0.88 us
  local copies, waits for them, and re-layouts: 18.9 us -> 5.96 us
  starting transfers between devices: 23.5 us -> 36.4 us
  blocking collectives: 29 us -> 34.5 us
    psum x1 -> x0, waiting for transfers between devices: 261 us -> none  [on_device(): lax.psum((spatial_term * grad_scale, temporal_term * grad_scale), DP_TILE)]
    ppermute x2 -> x8, waiting for transfers between devices: 1.49 us -> 41.2 us  [the longest x1 21.3 us: on_device(): above = lax.ppermute(bottom, TILE, [(i, i + 1) for i in range(ends)])]
    all_to_all x0 -> x2, blocking collectives: none -> 34.5 us  [share(): return lax.all_to_all(pieces, axes, 0, 0, tiled=True)]
    psum x2 -> x0, blocking collectives: 29 us -> none  [by_axis(): return functools.reduce(lax.psum, axes, shard)]
    pallas_call x0 -> x4, Pallas kernels: none -> 29 us  [the longest x1 15.6 us: on_device(): pl.pallas_call(functools.partial(forward_kernel, height), out_shape=(jax....]
    all_to_all x2 -> x3, waiting for transfers between devices: 6.26 us -> 27.2 us  [share(): return lax.all_to_all(pieces, axes, 0, 0, tiled=True)]
    dot_general x8 -> x0, matrix products: 19.8 us -> none  [the longest x2 12.7 us: contract_rows(): lax.dot_general(left, right, (((0,), (0,)), ((), ())), preferred_element_...]
    unnamed x47 -> x16, local copies, waits for them, and re-layouts: 14.8 us -> 3.63 us
  transfers between devices with their start and end apart: 5 -> 11, of which waited for: 4 -> 8; matrix products, arithmetic and copies ran while one was open for 8% -> 2% of each run, Pallas kernels for 0% -> 9%
where the time goes in v2:
time: 181 us; the launch traced here: 177 us
  waiting for transfers between devices  68.3 us (38%)
  starting transfers between devices  36.4 us (20%)
  blocking collectives  34.5 us (19%)
  Pallas kernels  29 us (16%)
  local copies, waits for them, and re-layouts  5.96 us (3%)
  other arithmetic  2.32 us (1%)
    all_to_all x2, blocking collectives, share(): return lax.all_to_all(pieces, axes, 0, 0, tiled=True)  34.5 us
    all_to_all x3, waiting for transfers between devices, share(): return lax.all_to_all(pieces, axes, 0, 0, tiled=True)  27.2 us
    all_to_all x3, starting transfers between devices, share(): return lax.all_to_all(pieces, axes, 0, 0, tiled=True)  21.7 us
    ppermute x1, waiting for transfers between devices, on_device(): above = lax.ppermute(bottom, TILE, [(i, i + 1) for i in range(ends)])  21.3 us
    ppermute x4, waiting for transfers between devices, on_device(): mine = stay + lax.ppermute(away, axes, pairs).astype(f32)  17.4 us
    pallas_call x1, Pallas kernels, on_device(): pl.pallas_call(functools.partial(forward_kernel, height), out_shape=(jax....  15.6 us
    pallas_call x1, Pallas kernels, on_device(): pl.pallas_call(functools.partial(backward_kernel, 1.0 / math.sqrt(pixel_t...  8.96 us
    ppermute x4, starting transfers between devices, on_device(): mine = stay + lax.ppermute(away, axes, pairs).astype(f32)  6.55 us
  transfers between devices with their start and end apart: 11, of which 8 were waited for; matrix products, arithmetic and copies ran while one was open for 2% of the time, Pallas kernels for 9%

profile of v2, /device:TPU:2, one launch (start us, length us, event | category | flops | bytes accessed | tf_op | source)
XLA Modules:
  0.0 177.3 jit_solution(1280701667468953931)
XLA Ops:
  0.6 0.0 copy-start
  0.6 1.2 copy-done
  1.9 0.0 copy-start.2
  1.9 0.7 copy-done.2
  2.5 2.0 %stats.1 = (f32[32,8,128]{2,1,0:T(8,128)}, bf16[64,8,256]{2,1,0:T(8,128)(2,1)S(1)}, bf16[64,8,256]{2,1,0:T(8,128)(2,1)S(1)}) custom-call(s32[1,6]{1,0:T(1,128)S(1)} %copy-done.2, bf16[64,4,8,256]{3,2,1,0:T(8,128)(2,1)S(1)} %bitcast.41), custom_call_target="tpu_custom_call" | custom-call | tf_op jit(solution)/shard_map/stats/pallas_call | solution.py:342
  4.5 11.6 %all-to-all-start = ((f32[32,8,128]{2,1,0:T(8,128)}), f32[32,8,128]{2,1,0:T(8,128)S(1)}, u32[]{:S(2)}, u32[]{:S(2)}) async-start(f32[32,8,128]{2,1,0:T(8,128)} %get-tuple-element.13), calls=%async_computation | async-start | bytes 262144 | tf_op jit(solution)/shard_map/all_to_all | solution.py:317
  16.2 0.0 copy-done.4
  16.2 1.1 copy.15
  17.2 8.0 %all-to-all-done.total_ref = f32[32,8,128]{2,1,0:T(8,128)S(1)} async-done(((f32[32,8,128]{2,1,0:T(8,128)}), f32[32,8,128]{2,1,0:T(8,128)S(1)}, u32[]{:S(2)}, u32[]{:S(2)}) %all-to-all-start) | async-done | bytes 131104 | tf_op jit(solution)/shard_map/all_to_all | solution.py:317
  25.3 5.0 %all-to-all-start.2 = ((bf16[32,2,4,8,256]{4,3,2,1,0:T(8,128)(2,1)}), bf16[32,2,4,8,256]{4,3,2,1,0:T(8,128)(2,1)S(1)}, u32[]{:S(2)}, u32[]{:S(2)}) async-start(bf16[32,2,4,8,256]{4,3,2,1,0:T(8,128)(2,1)} %bitcast.39), calls=%async_computation.2 | async-start | bytes 2097152 | tf_op jit(solution)/shard_map/all_to_all | solution.py:317
  30.3 3.4 %collective-permute-start = (bf16[64,8,256]{2,1,0:T(8,128)(2,1)S(1)}, bf16[64,8,256]{2,1,0:T(8,128)(2,1)S(1)}, u32[]{:S(2)}, u32[]{:S(2)}) collective-permute-start(bf16[64,8,256]{2,1,0:T(8,128)(2,1)S(1)} %get-tuple-element.14), channel_id=1, source_target_pairs={{0,1},{1,2},{2,3},{3,4},{4,5},{5,6},{6,7},{7,8},{8,9},{9,10},{10,1... | collective-permute-start | bytes 786440 | tf_op jit(solution)/shard_map/ppermute | solution.py:352
  33.7 4.6 %collective-permute-start.1 = (bf16[64,8,256]{2,1,0:T(8,128)(2,1)S(1)}, bf16[64,8,256]{2,1,0:T(8,128)(2,1)S(1)}, u32[]{:S(2)}, u32[]{:S(2)}) collective-permute-start(bf16[64,8,256]{2,1,0:T(8,128)(2,1)S(1)} %get-tuple-element.15), channel_id=1, source_target_pairs={{1,0},{2,1},{3,2},{4,3},{5,4},{6,5},{7,6},{8,7},{9,8},{10,9},{11,1... | collective-permute-start | bytes 786440 | tf_op jit(solution)/shard_map/ppermute | solution.py:353
  38.3 0.6 add_convert_fusion.place_ref
  38.8 21.3 %collective-permute-done.above_ref = bf16[64,8,256]{2,1,0:T(8,128)(2,1)S(1)} collective-permute-done((bf16[64,8,256]{2,1,0:T(8,128)(2,1)S(1)}, bf16[64,8,256]{2,1,0:T(8,128)(2,1)S(1)}, u32[]{:S(2)}, u32[]{:S(2)}) %collective-permute-start) | collective-permute-done | bytes 262176 | tf_op jit(solution)/shard_map/ppermute | solution.py:352
  60.2 0.0 collective-permute-done.1.below_ref
  60.2 0.0 copy-done.5
  60.2 0.7 copy-done.6
  60.9 0.1 copy-done.7
  60.9 15.6 %forward.1 = (bf16[64,4,8,256]{3,2,1,0:T(8,128)(2,1)}, bf16[6,512,768]{2,1,0:T(8,128)(2,1)}, bf16[4,512,256]{2,1,0:T(8,128)(2,1)}) custom-call(s32[1,6]{1,0:T(1,128)} %lengths_ref.5, s32[1,3]{1,0:T(1,128)} %add_convert_fusion.place_ref, f32[32,8,128]{2,1,0:T(8,128)} %copy-done.5, bf16[64,4,8,256]{3,2,1,0:T(8,128)(2,1)} %bitcast.40, ...), custom_call_target="tpu_custom_call" | custom-call | tf_op jit(solution)/shard_map/forward/pallas_call | solution.py:366
  76.5 0.0 all-to-all-done.2
  76.5 0.0 copy-start.3
  76.5 1.0 copy-done.3
  77.5 9.0 %backward.1 = (bf16[1536,256]{1,0:T(8,128)(2,1)}, f32[1536,256]{1,0:T(8,128)}) custom-call(s32[1,6]{1,0:T(1,128)} %lengths_ref.5, s32[1,3]{1,0:T(1,128)} %add_convert_fusion.place_ref, bf16[64,4,8,256]{3,2,1,0:T(8,128)(2,1)} %bitcast.47, bf16[3,256,256]{2,1,0:T(8,128)(2,1)} %weight_ref.1, bf16[6,512,768]{2,1,0:T(8,128)(2,1)} %get-tuple-element.17.kept_ref, ...), custom_call_target="tpu_custom_call" | custom-call | tf_op jit(solution)/shard_map/backward/pallas_call | solution.py:407
  86.5 0.1 collective-permute-start.2
  86.6 2.5 %collective-permute-done.2 = bf16[1536,256]{1,0:T(8,128)(2,1)S(1)} collective-permute-done((bf16[1536,256]{1,0:T(8,128)(2,1)}, bf16[1536,256]{1,0:T(8,128)(2,1)S(1)}, u32[]{:S(2)}, u32[]{:S(2)}) %collective-permute-start.2) | collective-permute-done | bytes 786464 | tf_op jit(solution)/shard_map/ppermute | solution.py:428
  89.1 1.6 convert_add_fusion
  90.6 0.1 fusion
  90.7 1.7 collective-permute-start.3
  92.3 6.2 %collective-permute-done.3 = bf16[768,256]{1,0:T(8,128)(2,1)S(1)} collective-permute-done((bf16[768,256]{1,0:T(8,128)(2,1)S(1)}, bf16[768,256]{1,0:T(8,128)(2,1)S(1)}, u32[]{:S(2)}, u32[]{:S(2)}) %collective-permute-start.3) | collective-permute-done | bytes 393248 | tf_op jit(solution)/shard_map/ppermute | solution.py:447
  98.6 0.1 bitcast_add_fusion
  98.7 3.3 %collective-permute-start.4 = (bf16[384,256]{1,0:T(8,128)(2,1)S(1)}, bf16[384,256]{1,0:T(8,128)(2,1)S(1)}, u32[]{:S(2)}, u32[]{:S(2)}) collective-permute-start(bf16[384,256]{1,0:T(8,128)(2,1)S(1)} %fusion.1), channel_id=1, source_target_pairs={{64,128},{128,64},{192,0},{0,192},{32,96},{96,32},{160,224},{224,1... | collective-permute-start | bytes 589832 | tf_op jit(solution)/shard_map/ppermute | solution.py:447
  101.9 3.9 %collective-permute-done.4 = bf16[384,256]{1,0:T(8,128)(2,1)S(1)} collective-permute-done((bf16[384,256]{1,0:T(8,128)(2,1)S(1)}, bf16[384,256]{1,0:T(8,128)(2,1)S(1)}, u32[]{:S(2)}, u32[]{:S(2)}) %collective-permute-start.4) | collective-permute-done | bytes 196640 | tf_op jit(solution)/shard_map/ppermute | solution.py:447
  105.9 0.1 collective-permute-start.5
  106.0 4.7 %collective-permute-done.5 = bf16[192,256]{1,0:T(8,128)(2,1)S(1)} collective-permute-done((bf16[192,256]{1,0:T(8,128)(2,1)S(1)}, bf16[192,256]{1,0:T(8,128)(2,1)S(1)}, u32[]{:S(2)}, u32[]{:S(2)}) %collective-permute-start.5) | collective-permute-done | bytes 98336 | tf_op jit(solution)/shard_map/ppermute | solution.py:447
  110.7 1.5 collective-permute-start.6
  112.2 2.6 %collective-permute-done.6 = bf16[96,256]{1,0:T(8,128)(2,1)S(1)} collective-permute-done((bf16[96,256]{1,0:T(8,128)(2,1)S(1)}, bf16[96,256]{1,0:T(8,128)(2,1)S(1)}, u32[]{:S(2)}, u32[]{:S(2)}) %collective-permute-start.6) | collective-permute-done | bytes 49184 | tf_op jit(solution)/shard_map/ppermute | solution.py:447
  114.9 16.4 %all_to_all.25 = bf16[8,96,256]{2,1,0:T(8,128)(2,1)S(1)} all-to-all(bf16[8,96,256]{2,1,0:T(8,128)(2,1)S(1)} %broadcast_in_dim.10), channel_id=1, replica_groups=mesh['row'=4,'core'=2,'tile_0'=4,'tile_1'=8] {'tile_1'}, dimensions={0} | all-to-all | bytes 786432 | tf_op jit(solution)/shard_map/all_to_all | solution.py:317
  131.4 0.1 reduce_sum.12
  131.4 0.1 broadcast_in_dim.22
  131.5 18.0 %all_to_all.26 = bf16[16,96,256]{2,1,0:T(8,128)(2,1)S(1)} all-to-all(bf16[16,96,256]{2,1,0:T(8,128)(2,1)S(1)} %broadcast_in_dim.22), channel_id=1, replica_groups=mesh['row'=4,'core'=2,'tile_0'=4,'tile_1'=8] {'row','tile_0'}, dimensions={0} | all-to-all | bytes 1572864 | tf_op jit(solution)/shard_map/all_to_all | solution.py:317
  149.5 5.1 %all-to-all-start.1 = ((bf16[32,2,4,8,256]{4,3,2,1,0:T(8,128)(2,1)}), bf16[32,2,4,8,256]{4,3,2,1,0:T(8,128)(2,1)S(1)}, u32[]{:S(2)}, u32[]{:S(2)}) async-start(bf16[32,2,4,8,256]{4,3,2,1,0:T(8,128)(2,1)} %bitcast.7), calls=%async_computation.1 | async-start | bytes 2097152 | tf_op jit(solution)/shard_map/all_to_all | solution.py:317
  154.6 0.0 copy-start.1
  154.6 0.1 collective-permute-start.7
  154.7 19.1 %all-to-all-done.1 = bf16[32,2,4,8,256]{4,3,2,1,0:T(8,128)(2,1)S(1)} async-done(((bf16[32,2,4,8,256]{4,3,2,1,0:T(8,128)(2,1)}), bf16[32,2,4,8,256]{4,3,2,1,0:T(8,128)(2,1)S(1)}, u32[]{:S(2)}, u32[]{:S(2)}) %all-to-all-start.1) | async-done | bytes 1048608 | tf_op jit(solution)/shard_map/all_to_all | solution.py:317
  173.9 1.1 copy.12
  174.9 0.0 collective-permute-done.7.facing_ref
  174.9 0.0 copy-done.1
  174.9 2.4 %finish.1 = (f32[2304,256]{1,0:T(8,128)}, f32[768,256]{1,0:T(8,128)}) custom-call(s32[1,3]{1,0:T(1,128)S(1)} %copy-done.1, bf16[1536,256]{1,0:T(8,128)(2,1)S(1)} %bitcast.43, bf16[1536,256]{1,0:T(8,128)(2,1)S(1)} %collective-permute-done.7.facing_ref), custom_call_target="tpu_custom_call" | custom-call | tf_op jit(solution)/shard_map/finish/pallas_call | solution.py:452
  (11 shorter events, 0.2 us)
Async XLA Ops:
  0.6 1.2 copy-start
  1.9 0.7 copy-start.2
  2.5 13.6 %copy-start.4 = (bf16[1,2,128,8,256]{4,3,2,1,0:T(8,128)(2,1)S(1)}, bf16[1,2,128,8,256]{4,3,2,1,0:T(8,128)(2,1)}, u32[]{:S(2)}) copy-start(bf16[1,2,128,8,256]{4,3,2,1,0:T(8,128)(2,1)} %param.13) | copy-start | bytes 3145732
  4.5 20.7 %all-to-all-start = ((f32[32,8,128]{2,1,0:T(8,128)}), f32[32,8,128]{2,1,0:T(8,128)S(1)}, u32[]{:S(2)}, u32[]{:S(2)}) async-start(f32[32,8,128]{2,1,0:T(8,128)} %get-tuple-element.13), calls=%async_computation | async-start | bytes 262144 | tf_op jit(solution)/shard_map/all_to_all | solution.py:317
  25.3 34.9 %copy-start.5 = (f32[32,8,128]{2,1,0:T(8,128)}, f32[32,8,128]{2,1,0:T(8,128)S(1)}, u32[]{:S(2)}) copy-start(f32[32,8,128]{2,1,0:T(8,128)S(1)} %all-to-all-done.total_ref) | copy-start | bytes 393220
  25.3 51.3 %all-to-all-start.2 = ((bf16[32,2,4,8,256]{4,3,2,1,0:T(8,128)(2,1)}), bf16[32,2,4,8,256]{4,3,2,1,0:T(8,128)(2,1)S(1)}, u32[]{:S(2)}, u32[]{:S(2)}) async-start(bf16[32,2,4,8,256]{4,3,2,1,0:T(8,128)(2,1)} %bitcast.39), calls=%async_computation.2 | async-start | bytes 2097152 | tf_op jit(solution)/shard_map/all_to_all | solution.py:317
  30.3 29.9 %collective-permute-start = (bf16[64,8,256]{2,1,0:T(8,128)(2,1)S(1)}, bf16[64,8,256]{2,1,0:T(8,128)(2,1)S(1)}, u32[]{:S(2)}, u32[]{:S(2)}) collective-permute-start(bf16[64,8,256]{2,1,0:T(8,128)(2,1)S(1)} %get-tuple-element.14), channel_id=1, source_target_pairs={{0,1},{1,2},{2,3},{3,4},{4,5},{5,6},{6,7},{7,8},{8,9},{9,10},{10,1... | collective-permute-start | bytes 786440 | tf_op jit(solution)/shard_map/ppermute | solution.py:352
  33.7 26.5 %collective-permute-start.1 = (bf16[64,8,256]{2,1,0:T(8,128)(2,1)S(1)}, bf16[64,8,256]{2,1,0:T(8,128)(2,1)S(1)}, u32[]{:S(2)}, u32[]{:S(2)}) collective-permute-start(bf16[64,8,256]{2,1,0:T(8,128)(2,1)S(1)} %get-tuple-element.15), channel_id=1, source_target_pairs={{1,0},{2,1},{3,2},{4,3},{5,4},{6,5},{7,6},{8,7},{9,8},{10,9},{11,1... | collective-permute-start | bytes 786440 | tf_op jit(solution)/shard_map/ppermute | solution.py:353
  60.2 0.7 copy-start.6
  60.2 0.8 copy-start.7
  76.5 1.0 copy-start.3
  86.5 2.6 %collective-permute-start.2 = (bf16[1536,256]{1,0:T(8,128)(2,1)}, bf16[1536,256]{1,0:T(8,128)(2,1)S(1)}, u32[]{:S(2)}, u32[]{:S(2)}) collective-permute-start(bf16[1536,256]{1,0:T(8,128)(2,1)} %get-tuple-element.20), channel_id=1, source_target_pairs={{0,32},{32,0},{1,33},{33,1},{2,34},{34,2},{3,35},{35,3},{4,36},{36... | collective-permute-start | bytes 2359304 | tf_op jit(solution)/shard_map/ppermute | solution.py:428
  90.7 7.9 %collective-permute-start.3 = (bf16[768,256]{1,0:T(8,128)(2,1)S(1)}, bf16[768,256]{1,0:T(8,128)(2,1)S(1)}, u32[]{:S(2)}, u32[]{:S(2)}) collective-permute-start(bf16[768,256]{1,0:T(8,128)(2,1)S(1)} %fusion), channel_id=1, source_target_pairs={{0,64},{64,0},{128,192},{192,128},{96,160},{160,96},{224,32},{32,2... | collective-permute-start | bytes 1179656 | tf_op jit(solution)/shard_map/ppermute | solution.py:447
  98.7 7.1 %collective-permute-start.4 = (bf16[384,256]{1,0:T(8,128)(2,1)S(1)}, bf16[384,256]{1,0:T(8,128)(2,1)S(1)}, u32[]{:S(2)}, u32[]{:S(2)}) collective-permute-start(bf16[384,256]{1,0:T(8,128)(2,1)S(1)} %fusion.1), channel_id=1, source_target_pairs={{64,128},{128,64},{192,0},{0,192},{32,96},{96,32},{160,224},{224,1... | collective-permute-start | bytes 589832 | tf_op jit(solution)/shard_map/ppermute | solution.py:447
  105.9 4.8 %collective-permute-start.5 = (bf16[192,256]{1,0:T(8,128)(2,1)S(1)}, bf16[192,256]{1,0:T(8,128)(2,1)S(1)}, u32[]{:S(2)}, u32[]{:S(2)}) collective-permute-start(bf16[192,256]{1,0:T(8,128)(2,1)S(1)} %fusion.2), channel_id=1, source_target_pairs={{0,8},{8,0},{16,24},{24,16},{40,48},{48,40},{56,32},{32,56},{1,9},... | collective-permute-start | bytes 294920 | tf_op jit(solution)/shard_map/ppermute | solution.py:447
  110.7 4.2 %collective-permute-start.6 = (bf16[96,256]{1,0:T(8,128)(2,1)S(1)}, bf16[96,256]{1,0:T(8,128)(2,1)S(1)}, u32[]{:S(2)}, u32[]{:S(2)}) collective-permute-start(bf16[96,256]{1,0:T(8,128)(2,1)S(1)} %fusion.4), channel_id=1, source_target_pairs={{8,16},{16,8},{24,0},{0,24},{32,40},{40,32},{48,56},{56,48},{9,17}... | collective-permute-start | bytes 147464 | tf_op jit(solution)/shard_map/ppermute | solution.py:447
  149.5 24.3 %all-to-all-start.1 = ((bf16[32,2,4,8,256]{4,3,2,1,0:T(8,128)(2,1)}), bf16[32,2,4,8,256]{4,3,2,1,0:T(8,128)(2,1)S(1)}, u32[]{:S(2)}, u32[]{:S(2)}) async-start(bf16[32,2,4,8,256]{4,3,2,1,0:T(8,128)(2,1)} %bitcast.7), calls=%async_computation.1 | async-start | bytes 2097152 | tf_op jit(solution)/shard_map/all_to_all | solution.py:317
  154.6 20.3 %copy-start.1 = (s32[1,3]{1,0:T(1,128)S(1)}, s32[1,3]{1,0:T(1,128)}, u32[]{:S(2)}) copy-start(s32[1,3]{1,0:T(1,128)} %add_convert_fusion.place_ref) | copy-start | bytes 40
  154.6 20.3 %collective-permute-start.7 = (bf16[1536,256]{1,0:T(8,128)(2,1)S(1)}, bf16[1536,256]{1,0:T(8,128)(2,1)S(1)}, u32[]{:S(2)}, u32[]{:S(2)}) collective-permute-start(bf16[1536,256]{1,0:T(8,128)(2,1)S(1)} %bitcast.42), channel_id=1, source_target_pairs={{0,32},{32,0},{1,33},{33,1},{2,34},{34,2},{3,35},{35,3},{4,36},{36... | collective-permute-start | bytes 2359304 | tf_op jit(solution)/shard_map/ppermute | solution.py:451

commit v3 on v2

v3 whole, which is shorter than its diff:
```python
import functools
import math

import jax
import jax.numpy as jnp
from jax import lax
from jax.experimental import pallas as pl
from jax.experimental.pallas import tpu as pltpu
from jax.sharding import Mesh
from jax.sharding import PartitionSpec as P


GROUPS = 32
PARTS = 3
SLOTS = 8
TILE = ("tile_0", "tile_1")
DP = ("row", "core")
PLANE = ("row", "tile_0")
MESH_AXES = ("row", "core", "tile_0", "tile_1")
SWAP = [(0, 1), (1, 0)]

norm_eps = 1e-05

VMEM = pl.BlockSpec(memory_space=pltpu.VMEM)
SMEM = pl.BlockSpec(memory_space=pltpu.SMEM)
HBM = pl.BlockSpec(memory_space=pltpu.HBM)
exact_dot = functools.partial(
    jnp.dot, precision=lax.Precision.HIGHEST, preferred_element_type=jnp.float32
)
dot = functools.partial(jnp.dot, preferred_element_type=jnp.float32)


def clip_starts(lengths_ref):
    starts = [jnp.int32(0)]
    for clip in range(lengths_ref.shape[1] - 1):
        starts.append(starts[-1] + lengths_ref[0, clip])
    return starts


def clip_of(starts, frame):
    clip = jnp.int32(0)
    first = jnp.int32(0)
    for number, start in enumerate(starts[1:], 1):
        inside = frame >= start
        clip = jnp.where(inside, number, clip)
        first = jnp.where(inside, start, first)
    return clip, first


def reach(starts, frame, steps, total):
    _, first = clip_of(starts, frame + steps)
    keep = (frame + steps < total) & (frame >= first)
    return jnp.where(keep, jnp.float32(1.0), jnp.float32(0.0))


def picker(rows, columns, offset, per_group, flip):
    row = lax.broadcasted_iota(jnp.int32, (rows, columns), 0)
    column = lax.broadcasted_iota(jnp.int32, (rows, columns), 1)
    lane, channel = (row, column) if flip else (column, row)
    lane_of = lane % (2 * GROUPS)
    match = (lane_of == channel // per_group + offset) & (lane < PARTS * 2 * GROUPS)
    return match.astype(jnp.float32)


def first_kernel(
    lengths_ref,
    video_ref,
    cot_ref,
    out_ref,
    top_ref,
    bottom_ref,
    video_in,
    sum_ref,
    square_ref,
    sems,
):
    held, _, rows, _, channels = cot_ref.shape
    frames = video_in.shape[0]
    loads = [pltpu.make_async_copy(video_ref, video_in, sems.at[0])]
    for frame in range(held):
        at = pl.ds(frame * rows, rows)
        loads.append(
            pltpu.make_async_copy(cot_ref.at[frame], out_ref.at[:, at], sems.at[1 + frame])
        )
    for load in loads:
        load.start()
    starts = clip_starts(lengths_ref)
    sum_ref[...] = jnp.zeros_like(sum_ref)
    square_ref[...] = jnp.zeros_like(square_ref)
    loads[0].wait()
    top_ref[...] = video_in[:, 0]
    bottom_ref[...] = video_in[:, rows - 1]

    def step(frame, carry):
        clip, _ = clip_of(starts, frame)
        cells = video_in[frame].astype(jnp.float32)
        sum_ref[clip] += jnp.sum(cells, axis=0)
        square_ref[clip] += jnp.sum(cells * cells, axis=0)
        return carry

    lax.fori_loop(0, frames, step, 0, unroll=4)
    per_group = channels // GROUPS
    sums = jnp.sum(sum_ref[...], axis=1)
    squares = jnp.sum(square_ref[...], axis=1)
    total = exact_dot(sums, picker(channels, channels, 0, per_group, False)) + exact_dot(
        squares, picker(channels, channels, GROUPS, per_group, False)
    )
    lane = lax.broadcasted_iota(jnp.int32, total.shape, 1)
    high = total.astype(jnp.bfloat16).astype(jnp.float32)
    middle = (total - high).astype(jnp.bfloat16).astype(jnp.float32)
    low = total - high - middle
    split = jnp.where(lane < 2 * GROUPS, high, jnp.where(lane < 4 * GROUPS, middle, low))
    split = split.astype(jnp.bfloat16)
    out_ref[:, held * rows] = jnp.broadcast_to(split[None], (out_ref.shape[0],) + split.shape)
    for load in loads[1:]:
        load.wait()


def column_shift(cells, step):
    column = lax.broadcasted_iota(jnp.int32, cells.shape, 1)
    width = cells.shape[1]
    edge = 0 if step == 1 else width - 1
    return jnp.where(column == edge, 0.0, pltpu.roll(cells, step % width, 1))


def main_kernel(
    height,
    grad_scale,
    lengths_ref,
    place_ref,
    moved_hbm,
    video_hbm,
    above_hbm,
    below_hbm,
    spatial_hbm,
    temporal_hbm,
    gain_ref,
    bias_ref,
    encoded_hbm,
    send_ref,
    keep_ref,
    moved_ref,
    video_ref,
    above_ref,
    below_ref,
    spatial_ref,
    temporal_ref,
    encoded_ref,
    mean_ref,
    scale_ref,
    active_ref,
    block_ref,
    stat_ref,
    earlier_ref,
    later_ref,
    grad_ref,
    wide_ref,
    part_ref,
    sems,
):
    frames, rows, width, channels = video_ref.shape
    per_group = channels // GROUPS
    cells = frames * width
    span = 3 * channels
    starts = clip_starts(lengths_ref)
    below_rows = moved_ref.shape[1]
    loads = [
        pltpu.make_async_copy(source, target, sems.at[number])
        for number, (source, target) in enumerate(
            (
                (moved_hbm.at[:, below_rows], stat_ref),
                (video_hbm, video_ref),
                (above_hbm, above_ref),
                (below_hbm, below_ref),
                (spatial_hbm, spatial_ref),
                (temporal_hbm, temporal_ref),
                (moved_hbm.at[:, pl.ds(0, below_rows)], moved_ref),
            )
        )
    ]
    for load in loads[:4]:
        load.start()

    loads[0].wait()
    total = jnp.sum(stat_ref[...].astype(jnp.float32), axis=0)
    sums = exact_dot(total, picker(channels, channels, 0, per_group, True))
    squares = exact_dot(total, picker(channels, channels, GROUPS, per_group, True))
    slot = lax.broadcasted_iota(jnp.int32, sums.shape, 0)
    counts = jnp.ones_like(sums)
    for clip in range(lengths_ref.shape[1]):
        in_clip = lengths_ref[0, clip].astype(jnp.float32) * (height * width * per_group)
        counts = jnp.where(slot == clip, in_clip, counts)
    mean = sums / counts
    var = jnp.maximum(squares / counts - mean * mean, 0.0)
    mean_ref[...] = mean
    scale_ref[...] = lax.rsqrt(var + norm_eps) * gain_ref[...]

    bias = bias_ref[...][None]
    has_above = place_ref[0, 0].astype(jnp.float32)
    has_below = place_ref[0, 1].astype(jnp.float32)
    for load in loads[1:4]:
        load.wait()
    for load in loads[4:]:
        load.start()

    def normalise(pair, carry):
        shifted = [[], [], []]
        for half in range(2):
            frame = pair * 2 + half
            clip, _ = clip_of(starts, frame)
            mean_row = mean_ref[pl.ds(clip, 1), :][None]
            scale_row = scale_ref[pl.ds(clip, 1), :][None]

            def activate(piece):
                normed = (piece.astype(jnp.float32) - mean_row) * scale_row + bias
                return normed * 0.5 * (1.0 + jnp.tanh(normed * 0.5))

            active = jnp.concatenate(
                [
                    activate(above_ref[frame][None]) * has_above,
                    activate(video_ref[frame]),
                    activate(below_ref[frame][None]) * has_below,
                ],
                axis=0,
            )
            active = active.astype(jnp.bfloat16).astype(jnp.float32)
            shifted[0].append(column_shift(active, 1))
            shifted[1].append(active)
            shifted[2].append(column_shift(active, -1))
        at = pl.ds(pl.multiple_of(pair * 2 * width, 2 * width), 2 * width)
        for j in range(3):
            active_ref[:, at, j * channels : (j + 1) * channels] = jnp.concatenate(
                shifted[j], axis=1
            ).astype(jnp.bfloat16)
        return carry

    lax.fori_loop(0, frames // 2, normalise, 0)

    for load in loads[4:]:
        load.wait()
    for row in range(rows):
        conv = dot(active_ref[row], spatial_ref[0])
        conv += dot(active_ref[row + 1], spatial_ref[1])
        conv += dot(active_ref[row + 2], spatial_ref[2])
        video_row = video_ref[:, row].astype(jnp.float32).reshape(cells, channels)
        block_ref[row] = (video_row + conv).astype(jnp.bfloat16)

    def both_ways(pair, carry):
        pairs = 2 * width
        at = pl.ds(pl.multiple_of(pair * pairs, pairs), pairs)
        before = pl.ds(pl.multiple_of(jnp.maximum(pair - 1, 0) * pairs, pairs), pairs)
        following = jnp.minimum(pair + 1, frames // 2 - 1)
        ahead = [
            moved_ref[source, side * rows : (side + 1) * rows].astype(jnp.float32)
            for source in (pair, following)
            for side in range(2)
        ]
        behind = []
        for place in (before, at):
            two = block_ref[:, place, :].astype(jnp.float32)
            behind += [two[:, :width], two[:, width:]]
        for k in range(3):
            onward, back = [], []
            for half in range(2):
                frame = pair * 2 + half
                _, first = clip_of(starts, frame)
                keep = jnp.where(frame - first >= k, jnp.float32(1.0), jnp.float32(0.0))
                back.append(behind[2 + half - k] * keep if k else behind[2 + half])
                after = ahead[half + k]
                onward.append(after * reach(starts, frame, k, frames) if k else after)
            columns = slice(k * channels, (k + 1) * channels)
            earlier_ref[:, at, columns] = jnp.concatenate(back, axis=1).astype(jnp.bfloat16)
            later_ref[:, at, columns] = jnp.concatenate(onward, axis=1).astype(jnp.bfloat16)
        return carry

    lax.fori_loop(0, frames // 2, both_ways, 0)
    for row in range(rows):
        lifted = dot(earlier_ref[row], temporal_ref[...].reshape(span, channels))
        out = block_ref[row].astype(jnp.float32) + lifted
        encoded_ref[:, row] = out.reshape(frames, width, channels).astype(jnp.bfloat16)
    save = pltpu.make_async_copy(encoded_ref, encoded_hbm, sems.at[7])
    save.start()

    for k in range(3):
        wide_ref[k * channels : (k + 1) * channels, :] = (
            temporal_ref[k].astype(jnp.float32).T.astype(jnp.bfloat16)
        )
    for row in range(rows):
        pulled = dot(later_ref[row], wide_ref[...])
        grad_ref[row] = (later_ref[row, :, :channels].astype(jnp.float32) + pulled).astype(
            jnp.bfloat16
        )
    flip = functools.partial(
        lax.dot_general,
        dimension_numbers=(((0,), (0,)), ((), ())),
        preferred_element_type=jnp.float32,
    )
    later = later_ref[...].reshape(rows * cells, span)
    temporal = flip(block_ref[...].reshape(rows * cells, channels), later) * grad_scale
    for k in range(3):
        part_ref[1, span + k * channels : span + (k + 1) * channels, :] = temporal[
            :, k * channels : (k + 1) * channels
        ]
    grads = grad_ref[...].reshape(rows * cells, channels)
    for i in range(3):
        tap = flip(grads, active_ref[i : i + rows].reshape(rows * cells, span)) * grad_scale
        part_ref[i // 2, (i % 2) * span : (i % 2 + 1) * span, :] = tap.T
    core = place_ref[0, 2]
    send_ref[...] = part_ref[1 - core].astype(jnp.bfloat16)
    keep_ref[...] = part_ref[core]
    save.wait()


def finish_kernel(place_ref, whole_ref, facing_ref, spatial_ref, temporal_ref):
    held = spatial_ref.shape[0]
    pieces = 16
    size = whole_ref.shape[0] // pieces
    turn, upper = (0, 1, 1, 0), (0, 0, 1, 1)

    def fill(side, source_ref):
        one, two = (turn, upper) if side == 0 else (upper, turn)
        for number in range(pieces):
            a, b = divmod(number, 4)
            spot = one[a] * 8 + two[a] * 4 + b
            at = (side * pieces + spot) * size
            piece = source_ref[number * size : (number + 1) * size, :].astype(jnp.float32)
            if at < held:
                spatial_ref[at : at + size, :] = piece
            else:
                temporal_ref[at - held : at - held + size, :] = piece

    @pl.when(place_ref[0, 2] == 0)
    def _():
        fill(0, whole_ref)
        fill(1, facing_ref)

    @pl.when(place_ref[0, 2] != 0)
    def _():
        fill(1, whole_ref)
        fill(0, facing_ref)


def share(pieces, axes):
    return lax.all_to_all(pieces, axes, 0, 0, tiled=True)


def copies(piece, axes):
    return jnp.broadcast_to(piece[None], (lax.axis_size(axes),) + piece.shape)


def summed(pieces):
    return jnp.sum(pieces.astype(jnp.float32), axis=0).astype(jnp.bfloat16)


def on_device(
    video_in, clip_lengths, norm_gain, norm_bias, spatial_weight, temporal_weight, cotangent
):
    tile_count = lax.axis_size(TILE)
    tile_index = lax.axis_index(TILE)
    video = video_in[0]
    frames, strip_rows, width, channels = video.shape
    height = strip_rows * tile_count
    span = 3 * channels
    cells = frames * width
    params = functools.partial(pltpu.CompilerParams, vmem_limit_bytes=24 * 1024 * 1024)
    f32, bf16 = jnp.float32, jnp.bfloat16

    held = frames // tile_count
    edge = jax.ShapeDtypeStruct((frames, width, channels), bf16)
    parcel, top, bottom = pl.pallas_call(
        first_kernel,
        out_shape=(
            jax.ShapeDtypeStruct((tile_count, held * strip_rows + 1, SLOTS, channels), bf16),
            edge,
            edge,
        ),
        in_specs=[SMEM, HBM, HBM],
        out_specs=(VMEM, VMEM, VMEM),
        scratch_shapes=[
            pltpu.VMEM(video.shape, bf16),
            pltpu.VMEM((SLOTS, width, channels), f32),
            pltpu.VMEM((SLOTS, width, channels), f32),
            pltpu.SemaphoreType.DMA((1 + held,)),
        ],
        compiler_params=params(vmem_limit_bytes=60 << 20),
        name="first",
    )(
        clip_lengths,
        video,
        cotangent[0].reshape(held, tile_count, strip_rows, width, channels),
    )
    ends = tile_count - 1
    above = lax.ppermute(bottom, TILE, [(i, i + 1) for i in range(ends)])
    below = lax.ppermute(top, TILE, [(i + 1, i) for i in range(ends)])
    moved = share(parcel, TILE)

    place = jnp.stack(
        [tile_index > 0, tile_index < tile_count - 1, lax.axis_index("core") > 0]
    ).astype(jnp.int32)[None]

    pixel_total = lax.axis_size(DP) * frames * height * width
    half_rows = 2 * span
    encoded_rows, send, keep = pl.pallas_call(
        functools.partial(main_kernel, height, 1.0 / math.sqrt(pixel_total)),
        out_shape=(
            jax.ShapeDtypeStruct((frames, strip_rows, width, channels), bf16),
            jax.ShapeDtypeStruct((half_rows, channels), bf16),
            jax.ShapeDtypeStruct((half_rows, channels), f32),
        ),
        in_specs=[SMEM, SMEM] + [HBM] * 6 + [VMEM, VMEM],
        out_specs=(HBM, VMEM, VMEM),
        scratch_shapes=[
            pltpu.VMEM((tile_count, held * strip_rows, width, channels), bf16),
            pltpu.VMEM(video.shape, bf16),
            pltpu.VMEM(above.shape, bf16),
            pltpu.VMEM(below.shape, bf16),
            pltpu.VMEM((3, span, channels), bf16),
            pltpu.VMEM((3, channels, channels), bf16),
            pltpu.VMEM(video.shape, bf16),
            pltpu.VMEM((SLOTS, channels), f32),
            pltpu.VMEM((SLOTS, channels), f32),
            pltpu.VMEM((strip_rows + 2, cells, span), bf16),
            pltpu.VMEM((strip_rows, cells, channels), bf16),
            pltpu.VMEM((tile_count, SLOTS, channels), bf16),
            pltpu.VMEM((strip_rows, cells, span), bf16),
            pltpu.VMEM((strip_rows, cells, span), bf16),
            pltpu.VMEM((strip_rows, cells, channels), bf16),
            pltpu.VMEM((span, channels), bf16),
            pltpu.VMEM((2, half_rows, channels), f32),
            pltpu.SemaphoreType.DMA((8,)),
        ],
        compiler_params=params(vmem_limit_bytes=60 << 20),
        name="main",
    )(
        clip_lengths,
        place,
        moved,
        video,
        above,
        below,
        spatial_weight.reshape(3, span, channels),
        temporal_weight,
        norm_gain[None],
        norm_bias[None],
    )
    encoded = share(
        encoded_rows.reshape(tile_count, held, strip_rows, width, channels), TILE
    )
    encoded = jnp.transpose(encoded, (1, 0, 2, 3, 4)).reshape(cotangent.shape)

    core = lax.axis_index("core")
    mine = keep + lax.ppermute(send, "core", SWAP).astype(f32)
    even = [(0, 1), (1, 0), (2, 3), (3, 2)]
    odd = [(1, 2), (2, 1), (3, 0), (0, 3)]
    spot = lax.axis_index("row")
    turn = jnp.where((spot == 1) | (spot == 2), 1, 0)
    upper = jnp.where(spot >= 2, 1, 0)
    for step in range(2):
        side = jnp.where(core == step, turn, upper)
        one, two = (even, odd) if step == 0 else (odd, even)
        pairs = [(2 * a, 2 * b) for a, b in one] + [(2 * a + 1, 2 * b + 1) for a, b in two]
        sides = mine.reshape(2, -1, channels)
        away = lax.dynamic_index_in_dim(sides, 1 - side, 0, keepdims=False).astype(bf16)
        stay = lax.dynamic_index_in_dim(sides, side, 0, keepdims=False)
        mine = stay + lax.ppermute(away, DP, pairs).astype(f32)
    count = lax.axis_size("tile_0")
    spot = lax.axis_index("tile_0")
    sides = mine.reshape(count, -1, channels)
    mine = lax.dynamic_index_in_dim(sides, spot, 0, keepdims=False)
    for step in (2, 1, 3):
        away = lax.dynamic_index_in_dim(sides, (spot + step) % count, 0, keepdims=False)
        pairs = [(k, (k + step) % count) for k in range(count)]
        mine += lax.ppermute(away.astype(bf16), "tile_0", pairs).astype(f32)
    pieces = share(copies(mine.astype(bf16), "tile_1"), "tile_1")
    piece = summed(pieces)
    whole = share(copies(piece, PLANE), PLANE).reshape(half_rows, channels)
    facing = lax.ppermute(whole, "core", SWAP)
    spatial_grad, temporal_grad = pl.pallas_call(
        finish_kernel,
        out_shape=(
            jax.ShapeDtypeStruct((3 * span, channels), f32),
            jax.ShapeDtypeStruct((span, channels), f32),
        ),
        in_specs=[SMEM, VMEM, VMEM],
        out_specs=(VMEM, VMEM),
        compiler_params=params(),
        name="finish",
    )(place, whole, facing)
    return (
        encoded,
        spatial_grad.reshape(3, 3, channels, channels),
        temporal_grad.reshape(3, channels, channels),
    )


def solution(mesh):
    finer = Mesh(mesh.devices.reshape(mesh.shape["dp"] // 2, 2, 4, 8), MESH_AXES)
    in_specs = (
        P(DP, None, TILE, None, None),
        P(DP, None),
        P(),
        P(),
        P(),
        P(),
        P(DP, TILE, None, None, None),
    )
    out_specs = (P(DP, TILE, None, None, None), P(), P())
    return jax.shard_map(
        on_device, mesh=finer, in_specs=in_specs, out_specs=out_specs, check_vma=False
    )
```

time: 181 us -> 158 us (0.87)
  Pallas kernels: 29 us -> 20.9 us
  waiting for transfers between devices: 68.3 us -> 60.8 us
  local copies, waits for them, and re-layouts: 5.96 us -> 2.47 us
  starting transfers between devices: 36.4 us -> 34.3 us
    pallas_call x3 -> x2, Pallas kernels: 26.5 us -> 18.5 us  [the longest x1 14.4 us: on_device(): pl.pallas_call(functools.partial(main_kernel, height, 1.0 / math.sqrt(pix...]
    all_to_all x3 -> x2, waiting for transfers between devices: 27.2 us -> 19.8 us  [share(): return lax.all_to_all(pieces, axes, 0, 0, tiled=True)]
    all_to_all x3 -> x2, starting transfers between devices: 21.7 us -> 16.9 us  [share(): return lax.all_to_all(pieces, axes, 0, 0, tiled=True)]
    ppermute x4 -> x5, waiting for transfers between devices: 17.4 us -> 13.3 us  [the longest x2 10.1 us: on_device(): mine = stay + lax.ppermute(away, DP, pairs).astype(f32)]
    ppermute x1, waiting for transfers between devices: 21.3 us -> 25.2 us  [on_device(): above = lax.ppermute(bottom, TILE, [(i, i + 1) for i in range(ends)])]
    ppermute x4 -> x5, starting transfers between devices: 6.55 us -> 9.26 us  [the longest x2 4.75 us: on_device(): mine = stay + lax.ppermute(away, DP, pairs).astype(f32)]
    unnamed x16 -> x12, local copies, waits for them, and re-layouts: 3.63 us -> 1.21 us
  transfers between devices with their start and end apart: 11 -> 11, of which waited for: 8 -> 8; matrix products, arithmetic and copies ran while one was open for 2% -> 1% of each run, Pallas kernels for 9% -> 0%
where the time goes in v3:
time: 158 us; the launch traced here: 155 us
  waiting for transfers between devices  60.8 us (38%)
  starting transfers between devices  34.3 us (22%)
  blocking collectives  32.9 us (21%)
  Pallas kernels  20.9 us (13%)
  local copies, waits for them, and re-layouts  2.47 us (2%)
  other arithmetic  2.31 us (1%)
    all_to_all x2, blocking collectives, share(): return lax.all_to_all(pieces, axes, 0, 0, tiled=True)  32.9 us
    ppermute x1, waiting for transfers between devices, on_device(): above = lax.ppermute(bottom, TILE, [(i, i + 1) for i in range(ends)])  25.2 us
    all_to_all x2, waiting for transfers between devices, share(): return lax.all_to_all(pieces, axes, 0, 0, tiled=True)  19.8 us
    all_to_all x2, starting transfers between devices, share(): return lax.all_to_all(pieces, axes, 0, 0, tiled=True)  16.9 us
    pallas_call x1, Pallas kernels, on_device(): pl.pallas_call(functools.partial(main_kernel, height, 1.0 / math.sqrt(pix...  14.4 us
    ppermute x2, waiting for transfers between devices, on_device(): mine = stay + lax.ppermute(away, DP, pairs).astype(f32)  10.1 us
    ppermute x2, starting transfers between devices, on_device(): mine = stay + lax.ppermute(away, DP, pairs).astype(f32)  4.75 us
    ppermute x1, starting transfers between devices, on_device(): below = lax.ppermute(top, TILE, [(i + 1, i) for i in range(ends)])  4.58 us
  transfers between devices with their start and end apart: 11, of which 8 were waited for; matrix products, arithmetic and copies ran while one was open for 1% of the time, Pallas kernels for 0%

profile of v3, /device:TPU:2, one launch (start us, length us, event | category | flops | bytes accessed | tf_op | source)
XLA Modules:
  0.0 154.5 jit_solution(6118936913607449830)
XLA Ops:
  0.6 4.1 %first.1 = (bf16[32,9,8,256]{3,2,1,0:T(8,128)(2,1)}, bf16[64,8,256]{2,1,0:T(8,128)(2,1)}, bf16[64,8,256]{2,1,0:T(8,128)(2,1)}) custom-call(s32[1,6]{1,0:T(1,128)} %lengths_ref.3, bf16[64,4,8,256]{3,2,1,0:T(8,128)(2,1)} %bitcast.43, bf16[2,32,4,8,256]{4,3,2,1,0:T(8,128)(2,1)} %bitcast.49), custom_call_target="tpu_custom_call" | custom-call | tf_op jit(solution)/shard_map/first/pallas_call | solution.py:370
  4.7 0.0 copy-start.5
  4.7 0.0 copy-start.4
  4.7 11.8 %all-to-all-start = ((bf16[32,9,8,256]{3,2,1,0:T(8,128)(2,1)}), bf16[32,9,8,256]{3,2,1,0:T(8,128)(2,1)S(1)}, u32[]{:S(2)}, u32[]{:S(2)}) async-start(bf16[32,9,8,256]{3,2,1,0:T(8,128)(2,1)} %get-tuple-element.11), calls=%async_computation | async-start | bytes 2359296 | tf_op jit(solution)/shard_map/all_to_all | solution.py:344
  16.5 0.0 copy-done.5
  16.5 3.4 %collective-permute-start = (bf16[64,8,256]{2,1,0:T(8,128)(2,1)S(1)}, bf16[64,8,256]{2,1,0:T(8,128)(2,1)S(1)}, u32[]{:S(2)}, u32[]{:S(2)}) collective-permute-start(bf16[64,8,256]{2,1,0:T(8,128)(2,1)S(1)} %copy-done.5), channel_id=1, source_target_pairs={{0,1},{1,2},{2,3},{3,4},{4,5},{5,6},{6,7},{7,8},{8,9},{9,10},{10,1... | collective-permute-start | bytes 786440 | tf_op jit(solution)/shard_map/ppermute | solution.py:393
  19.9 0.0 copy-done.4
  19.9 4.6 %collective-permute-start.1 = (bf16[64,8,256]{2,1,0:T(8,128)(2,1)S(1)}, bf16[64,8,256]{2,1,0:T(8,128)(2,1)S(1)}, u32[]{:S(2)}, u32[]{:S(2)}) collective-permute-start(bf16[64,8,256]{2,1,0:T(8,128)(2,1)S(1)} %copy-done.4), channel_id=1, source_target_pairs={{1,0},{2,1},{3,2},{4,3},{5,4},{6,5},{7,6},{8,7},{9,8},{10,9},{11,1... | collective-permute-start | bytes 786440 | tf_op jit(solution)/shard_map/ppermute | solution.py:394
  24.5 0.6 add_convert_fusion.place_ref
  25.1 25.2 %collective-permute-done.above_hbm = bf16[64,8,256]{2,1,0:T(8,128)(2,1)S(1)} collective-permute-done((bf16[64,8,256]{2,1,0:T(8,128)(2,1)S(1)}, bf16[64,8,256]{2,1,0:T(8,128)(2,1)S(1)}, u32[]{:S(2)}, u32[]{:S(2)}) %collective-permute-start) | collective-permute-done | bytes 262176 | tf_op jit(solution)/shard_map/ppermute | solution.py:393
  50.3 0.0 copy-start.2
  50.3 0.0 collective-permute-done.1.below_hbm
  50.3 0.0 copy-start.3
  50.3 0.0 all-to-all-done.moved_hbm
  50.3 0.0 copy-start.1
  50.3 0.7 copy-done.2
  51.0 0.1 copy-done.3
  51.1 0.4 copy-done.1
  51.5 14.4 %main.1 = (bf16[64,4,8,256]{3,2,1,0:T(8,128)(2,1)}, bf16[1536,256]{1,0:T(8,128)(2,1)}, f32[1536,256]{1,0:T(8,128)}) custom-call(s32[1,6]{1,0:T(1,128)} %lengths_ref.3, s32[1,3]{1,0:T(1,128)} %add_convert_fusion.place_ref, bf16[32,9,8,256]{3,2,1,0:T(8,128)(2,1)} %copy-done.1, bf16[64,4,8,256]{3,2,1,0:T(8,128)(2,1)} %bitcast.44, ...), custom_call_target="tpu_custom_call" | custom-call | tf_op jit(solution)/shard_map/main/pallas_call | solution.py:403
  66.0 0.1 collective-permute-start.2
  66.1 2.5 %collective-permute-done.2 = bf16[1536,256]{1,0:T(8,128)(2,1)S(1)} collective-permute-done((bf16[1536,256]{1,0:T(8,128)(2,1)}, bf16[1536,256]{1,0:T(8,128)(2,1)S(1)}, u32[]{:S(2)}, u32[]{:S(2)}) %collective-permute-start.2) | collective-permute-done | bytes 786464 | tf_op jit(solution)/shard_map/ppermute | solution.py:452
  68.5 1.6 %convert_add_fusion = f32[1536,256]{1,0:T(8,128)S(1)} fusion(f32[1536,256]{1,0:T(8,128)} %get-tuple-element.15, bf16[1536,256]{1,0:T(8,128)(2,1)S(1)} %collective-permute-done.2), kind=kLoop, calls=%fused_computation | loop fusion | flops 786432 | bytes 3932160 | tf_op jit(solution)/shard_map/add | solution.py:452
  70.1 0.1 fusion
  70.2 1.7 %collective-permute-start.3 = (bf16[768,256]{1,0:T(8,128)(2,1)S(1)}, bf16[768,256]{1,0:T(8,128)(2,1)S(1)}, u32[]{:S(2)}, u32[]{:S(2)}) collective-permute-start(bf16[768,256]{1,0:T(8,128)(2,1)S(1)} %fusion), channel_id=1, source_target_pairs={{0,64},{64,0},{128,192},{192,128},{96,160},{160,96},{224,32},{32,2... | collective-permute-start | bytes 1179656 | tf_op jit(solution)/shard_map/ppermute | solution.py:465
  71.8 6.2 %collective-permute-done.3 = bf16[768,256]{1,0:T(8,128)(2,1)S(1)} collective-permute-done((bf16[768,256]{1,0:T(8,128)(2,1)S(1)}, bf16[768,256]{1,0:T(8,128)(2,1)S(1)}, u32[]{:S(2)}, u32[]{:S(2)}) %collective-permute-start.3) | collective-permute-done | bytes 393248 | tf_op jit(solution)/shard_map/ppermute | solution.py:465
  78.0 0.1 bitcast_add_fusion
  78.2 3.1 %collective-permute-start.4 = (bf16[384,256]{1,0:T(8,128)(2,1)S(1)}, bf16[384,256]{1,0:T(8,128)(2,1)S(1)}, u32[]{:S(2)}, u32[]{:S(2)}) collective-permute-start(bf16[384,256]{1,0:T(8,128)(2,1)S(1)} %fusion.1), channel_id=1, source_target_pairs={{64,128},{128,64},{192,0},{0,192},{32,96},{96,32},{160,224},{224,1... | collective-permute-start | bytes 589832 | tf_op jit(solution)/shard_map/ppermute | solution.py:465
  81.3 3.9 %collective-permute-done.4 = bf16[384,256]{1,0:T(8,128)(2,1)S(1)} collective-permute-done((bf16[384,256]{1,0:T(8,128)(2,1)S(1)}, bf16[384,256]{1,0:T(8,128)(2,1)S(1)}, u32[]{:S(2)}, u32[]{:S(2)}) %collective-permute-start.4) | collective-permute-done | bytes 196640 | tf_op jit(solution)/shard_map/ppermute | solution.py:465
  85.2 2.5 %collective-permute-start.5 = (bf16[96,256]{1,0:T(8,128)(2,1)S(1)}, bf16[96,256]{1,0:T(8,128)(2,1)S(1)}, u32[]{:S(2)}, u32[]{:S(2)}) collective-permute-start(bf16[96,256]{1,0:T(8,128)(2,1)S(1)} %get-tuple-element.19), channel_id=1, source_target_pairs={{0,16},{8,24},{16,0},{24,8},{1,17},{9,25},{17,1},{25,9},{2,18},{10... | collective-permute-start | bytes 147464 | tf_op jit(solution)/shard_map/ppermute | solution.py:473
  87.7 1.1 collective-permute-start.7
  88.8 0.9 collective-permute-start.6
  89.7 1.2 collective-permute-done.5
  90.9 0.9 collective-permute-done.7
  91.8 1.1 collective-permute-done.6
  93.0 16.2 %all_to_all.20 = bf16[8,96,256]{2,1,0:T(8,128)(2,1)S(1)} all-to-all(bf16[8,96,256]{2,1,0:T(8,128)(2,1)S(1)} %broadcast_in_dim.10), channel_id=1, replica_groups=mesh['row'=4,'core'=2,'tile_0'=4,'tile_1'=8] {'tile_1'}, dimensions={0} | all-to-all | bytes 786432 | tf_op jit(solution)/shard_map/all_to_all | solution.py:344
  109.2 0.1 reduce_sum.12
  109.3 0.1 broadcast_in_dim.22
  109.3 16.6 %all_to_all.21 = bf16[16,96,256]{2,1,0:T(8,128)(2,1)S(1)} all-to-all(bf16[16,96,256]{2,1,0:T(8,128)(2,1)S(1)} %broadcast_in_dim.22), channel_id=1, replica_groups=mesh['row'=4,'core'=2,'tile_0'=4,'tile_1'=8] {'row','tile_0'}, dimensions={0} | all-to-all | bytes 1572864 | tf_op jit(solution)/shard_map/all_to_all | solution.py:344
  126.0 5.1 %all-to-all-start.1 = ((bf16[32,2,4,8,256]{4,3,2,1,0:T(8,128)(2,1)}), bf16[32,2,4,8,256]{4,3,2,1,0:T(8,128)(2,1)S(1)}, u32[]{:S(2)}, u32[]{:S(2)}) async-start(bf16[32,2,4,8,256]{4,3,2,1,0:T(8,128)(2,1)} %bitcast.8), calls=%async_computation.1 | async-start | bytes 2097152 | tf_op jit(solution)/shard_map/all_to_all | solution.py:344
  131.1 0.0 copy-start
  131.1 0.1 collective-permute-start.8
  131.2 19.8 %all-to-all-done.1 = bf16[32,2,4,8,256]{4,3,2,1,0:T(8,128)(2,1)S(1)} async-done(((bf16[32,2,4,8,256]{4,3,2,1,0:T(8,128)(2,1)}), bf16[32,2,4,8,256]{4,3,2,1,0:T(8,128)(2,1)S(1)}, u32[]{:S(2)}, u32[]{:S(2)}) %all-to-all-start.1) | async-done | bytes 1048608 | tf_op jit(solution)/shard_map/all_to_all | solution.py:344
  151.0 1.1 copy.11
  152.1 0.0 collective-permute-done.8.facing_ref
  152.1 0.0 copy-done
  152.1 2.4 %finish.1 = (f32[2304,256]{1,0:T(8,128)}, f32[768,256]{1,0:T(8,128)}) custom-call(s32[1,3]{1,0:T(1,128)S(1)} %copy-done, bf16[1536,256]{1,0:T(8,128)(2,1)S(1)} %bitcast.40, bf16[1536,256]{1,0:T(8,128)(2,1)S(1)} %collective-permute-done.8.facing_ref), custom_call_target="tpu_custom_call" | custom-call | tf_op jit(solution)/shard_map/finish/pallas_call | solution.py:478
  (5 shorter events, 0.1 us)
Async XLA Ops:
  4.7 11.8 %copy-start.5 = (bf16[64,8,256]{2,1,0:T(8,128)(2,1)S(1)}, bf16[64,8,256]{2,1,0:T(8,128)(2,1)}, u32[]{:S(2)}) copy-start(bf16[64,8,256]{2,1,0:T(8,128)(2,1)} %get-tuple-element.12) | copy-start | bytes 786436
  4.7 15.2 %copy-start.4 = (bf16[64,8,256]{2,1,0:T(8,128)(2,1)S(1)}, bf16[64,8,256]{2,1,0:T(8,128)(2,1)}, u32[]{:S(2)}) copy-start(bf16[64,8,256]{2,1,0:T(8,128)(2,1)} %get-tuple-element.13) | copy-start | bytes 786436
  4.7 45.6 %all-to-all-start = ((bf16[32,9,8,256]{3,2,1,0:T(8,128)(2,1)}), bf16[32,9,8,256]{3,2,1,0:T(8,128)(2,1)S(1)}, u32[]{:S(2)}, u32[]{:S(2)}) async-start(bf16[32,9,8,256]{3,2,1,0:T(8,128)(2,1)} %get-tuple-element.11), calls=%async_computation | async-start | bytes 2359296 | tf_op jit(solution)/shard_map/all_to_all | solution.py:344
  16.5 33.8 %collective-permute-start = (bf16[64,8,256]{2,1,0:T(8,128)(2,1)S(1)}, bf16[64,8,256]{2,1,0:T(8,128)(2,1)S(1)}, u32[]{:S(2)}, u32[]{:S(2)}) collective-permute-start(bf16[64,8,256]{2,1,0:T(8,128)(2,1)S(1)} %copy-done.5), channel_id=1, source_target_pairs={{0,1},{1,2},{2,3},{3,4},{4,5},{5,6},{6,7},{7,8},{8,9},{9,10},{10,1... | collective-permute-start | bytes 786440 | tf_op jit(solution)/shard_map/ppermute | solution.py:393
  19.9 30.4 %collective-permute-start.1 = (bf16[64,8,256]{2,1,0:T(8,128)(2,1)S(1)}, bf16[64,8,256]{2,1,0:T(8,128)(2,1)S(1)}, u32[]{:S(2)}, u32[]{:S(2)}) collective-permute-start(bf16[64,8,256]{2,1,0:T(8,128)(2,1)S(1)} %copy-done.4), channel_id=1, source_target_pairs={{1,0},{2,1},{3,2},{4,3},{5,4},{6,5},{7,6},{8,7},{9,8},{10,9},{11,1... | collective-permute-start | bytes 786440 | tf_op jit(solution)/shard_map/ppermute | solution.py:394
  50.3 0.7 copy-start.2
  50.3 0.8 copy-start.3
  50.3 1.2 copy-start.1
  66.0 2.6 %collective-permute-start.2 = (bf16[1536,256]{1,0:T(8,128)(2,1)}, bf16[1536,256]{1,0:T(8,128)(2,1)S(1)}, u32[]{:S(2)}, u32[]{:S(2)}) collective-permute-start(bf16[1536,256]{1,0:T(8,128)(2,1)} %get-tuple-element.16), channel_id=1, source_target_pairs={{0,32},{32,0},{1,33},{33,1},{2,34},{34,2},{3,35},{35,3},{4,36},{36... | collective-permute-start | bytes 2359304 | tf_op jit(solution)/shard_map/ppermute | solution.py:452
  70.2 7.9 %collective-permute-start.3 = (bf16[768,256]{1,0:T(8,128)(2,1)S(1)}, bf16[768,256]{1,0:T(8,128)(2,1)S(1)}, u32[]{:S(2)}, u32[]{:S(2)}) collective-permute-start(bf16[768,256]{1,0:T(8,128)(2,1)S(1)} %fusion), channel_id=1, source_target_pairs={{0,64},{64,0},{128,192},{192,128},{96,160},{160,96},{224,32},{32,2... | collective-permute-start | bytes 1179656 | tf_op jit(solution)/shard_map/ppermute | solution.py:465
  78.2 7.0 %collective-permute-start.4 = (bf16[384,256]{1,0:T(8,128)(2,1)S(1)}, bf16[384,256]{1,0:T(8,128)(2,1)S(1)}, u32[]{:S(2)}, u32[]{:S(2)}) collective-permute-start(bf16[384,256]{1,0:T(8,128)(2,1)S(1)} %fusion.1), channel_id=1, source_target_pairs={{64,128},{128,64},{192,0},{0,192},{32,96},{96,32},{160,224},{224,1... | collective-permute-start | bytes 589832 | tf_op jit(solution)/shard_map/ppermute | solution.py:465
  85.2 5.7 %collective-permute-start.5 = (bf16[96,256]{1,0:T(8,128)(2,1)S(1)}, bf16[96,256]{1,0:T(8,128)(2,1)S(1)}, u32[]{:S(2)}, u32[]{:S(2)}) collective-permute-start(bf16[96,256]{1,0:T(8,128)(2,1)S(1)} %get-tuple-element.19), channel_id=1, source_target_pairs={{0,16},{8,24},{16,0},{24,8},{1,17},{9,25},{17,1},{25,9},{2,18},{10... | collective-permute-start | bytes 147464 | tf_op jit(solution)/shard_map/ppermute | solution.py:473
  87.7 4.1 %collective-permute-start.7 = (bf16[96,256]{1,0:T(8,128)(2,1)S(1)}, bf16[96,256]{1,0:T(8,128)(2,1)S(1)}, u32[]{:S(2)}, u32[]{:S(2)}) collective-permute-start(bf16[96,256]{1,0:T(8,128)(2,1)S(1)} %get-tuple-element.20), channel_id=1, source_target_pairs={{0,24},{8,0},{16,8},{24,16},{1,25},{9,1},{17,9},{25,17},{2,26},{10... | collective-permute-start | bytes 147464 | tf_op jit(solution)/shard_map/ppermute | solution.py:473
  88.8 4.1 %collective-permute-start.6 = (bf16[96,256]{1,0:T(8,128)(2,1)S(1)}, bf16[96,256]{1,0:T(8,128)(2,1)S(1)}, u32[]{:S(2)}, u32[]{:S(2)}) collective-permute-start(bf16[96,256]{1,0:T(8,128)(2,1)S(1)} %get-tuple-element.21), channel_id=1, source_target_pairs={{0,8},{8,16},{16,24},{24,0},{1,9},{9,17},{17,25},{25,1},{2,10},{10... | collective-permute-start | bytes 147464 | tf_op jit(solution)/shard_map/ppermute | solution.py:473
  126.0 25.0 %all-to-all-start.1 = ((bf16[32,2,4,8,256]{4,3,2,1,0:T(8,128)(2,1)}), bf16[32,2,4,8,256]{4,3,2,1,0:T(8,128)(2,1)S(1)}, u32[]{:S(2)}, u32[]{:S(2)}) async-start(bf16[32,2,4,8,256]{4,3,2,1,0:T(8,128)(2,1)} %bitcast.8), calls=%async_computation.1 | async-start | bytes 2097152 | tf_op jit(solution)/shard_map/all_to_all | solution.py:344
  131.1 21.0 %copy-start = (s32[1,3]{1,0:T(1,128)S(1)}, s32[1,3]{1,0:T(1,128)}, u32[]{:S(2)}) copy-start(s32[1,3]{1,0:T(1,128)} %add_convert_fusion.place_ref) | copy-start | bytes 40
  131.1 21.0 %collective-permute-start.8 = (bf16[1536,256]{1,0:T(8,128)(2,1)S(1)}, bf16[1536,256]{1,0:T(8,128)(2,1)S(1)}, u32[]{:S(2)}, u32[]{:S(2)}) collective-permute-start(bf16[1536,256]{1,0:T(8,128)(2,1)S(1)} %bitcast.39), channel_id=1, source_target_pairs={{0,32},{32,0},{1,33},{33,1},{2,34},{34,2},{3,35},{35,3},{4,36},{36... | collective-permute-start | bytes 2359304 | tf_op jit(solution)/shard_map/ppermute | solution.py:477

commit v4 on v3

--- a/solution.py
+++ b/solution.py
@@ -12,6 +12,7 @@
 
 GROUPS = 32
 PARTS = 3
+CHUNKS = 4
 SLOTS = 8
 TILE = ("tile_0", "tile_1")
 DP = ("row", "core")
@@ -76,20 +77,21 @@
 ):
     held, _, rows, _, channels = cot_ref.shape
     frames = video_in.shape[0]
-    loads = [pltpu.make_async_copy(video_ref, video_in, sems.at[0])]
+    loads = []
+    chunk = frames // CHUNKS
+    for number in range(CHUNKS):
+        at = pl.ds(number * chunk, chunk)
+        loads.append(pltpu.make_async_copy(video_ref.at[at], video_in.at[at], sems.at[number]))
     for frame in range(held):
         at = pl.ds(frame * rows, rows)
         loads.append(
-            pltpu.make_async_copy(cot_ref.at[frame], out_ref.at[:, at], sems.at[1 + frame])
+            pltpu.make_async_copy(cot_ref.at[frame], out_ref.at[:, at], sems.at[CHUNKS + frame])
         )
     for load in loads:
         load.start()
     starts = clip_starts(lengths_ref)
     sum_ref[...] = jnp.zeros_like(sum_ref)
     square_ref[...] = jnp.zeros_like(square_ref)
-    loads[0].wait()
-    top_ref[...] = video_in[:, 0]
-    bottom_ref[...] = video_in[:, rows - 1]
 
     def step(frame, carry):
         clip, _ = clip_of(starts, frame)
@@ -98,7 +100,12 @@
         square_ref[clip] += jnp.sum(cells * cells, axis=0)
         return carry
 
-    lax.fori_loop(0, frames, step, 0, unroll=4)
+    for number in range(CHUNKS):
+        loads[number].wait()
+        at = slice(number * chunk, (number + 1) * chunk)
+        top_ref[at] = video_in[at, 0]
+        bottom_ref[at] = video_in[at, rows - 1]
+        lax.fori_loop(number * chunk, (number + 1) * chunk, step, 0, unroll=4)
     per_group = channels // GROUPS
     sums = jnp.sum(sum_ref[...], axis=1)
     squares = jnp.sum(square_ref[...], axis=1)
@@ -112,7 +119,7 @@
     split = jnp.where(lane < 2 * GROUPS, high, jnp.where(lane < 4 * GROUPS, middle, low))
     split = split.astype(jnp.bfloat16)
     out_ref[:, held * rows] = jnp.broadcast_to(split[None], (out_ref.shape[0],) + split.shape)
-    for load in loads[1:]:
+    for load in loads[CHUNKS:]:
         load.wait()
 
 
@@ -380,7 +387,7 @@
             pltpu.VMEM(video.shape, bf16),
             pltpu.VMEM((SLOTS, width, channels), f32),
             pltpu.VMEM((SLOTS, width, channels), f32),
-            pltpu.SemaphoreType.DMA((1 + held,)),
+            pltpu.SemaphoreType.DMA((CHUNKS + held,)),
         ],
         compiler_params=params(vmem_limit_bytes=60 << 20),
         name="first",

time: 158 us -> 157 us (level)
  no operation moved by 1% of the time
where the time goes in v4:
time: 157 us; the launch traced here: 154 us
  waiting for transfers between devices  60.8 us (39%)
  starting transfers between devices  34.3 us (22%)
  blocking collectives  32.9 us (21%)
  Pallas kernels  20.7 us (13%)
  local copies, waits for them, and re-layouts  2.47 us (2%)
  other arithmetic  2.31 us (1%)
    all_to_all x2, blocking collectives, share(): return lax.all_to_all(pieces, axes, 0, 0, tiled=True)  32.9 us
    ppermute x1, waiting for transfers between devices, on_device(): above = lax.ppermute(bottom, TILE, [(i, i + 1) for i in range(ends)])  25.2 us
    all_to_all x2, waiting for transfers between devices, share(): return lax.all_to_all(pieces, axes, 0, 0, tiled=True)  19.8 us
    all_to_all x2, starting transfers between devices, share(): return lax.all_to_all(pieces, axes, 0, 0, tiled=True)  16.9 us
    pallas_call x1, Pallas kernels, on_device(): pl.pallas_call(functools.partial(main_kernel, height, 1.0 / math.sqrt(pix...  14.4 us
    ppermute x2, waiting for transfers between devices, on_device(): mine = stay + lax.ppermute(away, DP, pairs).astype(f32)  10.1 us
    ppermute x2, starting transfers between devices, on_device(): mine = stay + lax.ppermute(away, DP, pairs).astype(f32)  4.76 us
    ppermute x1, starting transfers between devices, on_device(): below = lax.ppermute(top, TILE, [(i + 1, i) for i in range(ends)])  4.58 us
  transfers between devices with their start and end apart: 11, of which 8 were waited for; matrix products, arithmetic and copies ran while one was open for 1% of the time, Pallas kernels for 0%

profile of v4, /device:TPU:2, one launch (start us, length us, event | category | flops | bytes accessed | tf_op | source)
XLA Modules:
  0.0 154.2 jit_solution(13127509740749187832)
XLA Ops:
  0.6 3.8 %first.1 = (bf16[32,9,8,256]{3,2,1,0:T(8,128)(2,1)}, bf16[64,8,256]{2,1,0:T(8,128)(2,1)}, bf16[64,8,256]{2,1,0:T(8,128)(2,1)}) custom-call(s32[1,6]{1,0:T(1,128)} %lengths_ref.3, bf16[64,4,8,256]{3,2,1,0:T(8,128)(2,1)} %bitcast.43, bf16[2,32,4,8,256]{4,3,2,1,0:T(8,128)(2,1)} %bitcast.49), custom_call_target="tpu_custom_call" | custom-call | tf_op jit(solution)/shard_map/first/pallas_call | solution.py:377
  4.4 0.0 copy-start.5
  4.5 0.0 copy-start.4
  4.5 11.8 %all-to-all-start = ((bf16[32,9,8,256]{3,2,1,0:T(8,128)(2,1)}), bf16[32,9,8,256]{3,2,1,0:T(8,128)(2,1)S(1)}, u32[]{:S(2)}, u32[]{:S(2)}) async-start(bf16[32,9,8,256]{3,2,1,0:T(8,128)(2,1)} %get-tuple-element.11), calls=%async_computation | async-start | bytes 2359296 | tf_op jit(solution)/shard_map/all_to_all | solution.py:351
  16.2 0.0 copy-done.5
  16.2 3.4 %collective-permute-start = (bf16[64,8,256]{2,1,0:T(8,128)(2,1)S(1)}, bf16[64,8,256]{2,1,0:T(8,128)(2,1)S(1)}, u32[]{:S(2)}, u32[]{:S(2)}) collective-permute-start(bf16[64,8,256]{2,1,0:T(8,128)(2,1)S(1)} %copy-done.5), channel_id=1, source_target_pairs={{0,1},{1,2},{2,3},{3,4},{4,5},{5,6},{6,7},{7,8},{8,9},{9,10},{10,1... | collective-permute-start | bytes 786440 | tf_op jit(solution)/shard_map/ppermute | solution.py:400
  19.6 0.0 copy-done.4
  19.6 4.6 %collective-permute-start.1 = (bf16[64,8,256]{2,1,0:T(8,128)(2,1)S(1)}, bf16[64,8,256]{2,1,0:T(8,128)(2,1)S(1)}, u32[]{:S(2)}, u32[]{:S(2)}) collective-permute-start(bf16[64,8,256]{2,1,0:T(8,128)(2,1)S(1)} %copy-done.4), channel_id=1, source_target_pairs={{1,0},{2,1},{3,2},{4,3},{5,4},{6,5},{7,6},{8,7},{9,8},{10,9},{11,1... | collective-permute-start | bytes 786440 | tf_op jit(solution)/shard_map/ppermute | solution.py:401
  24.2 0.6 add_convert_fusion.place_ref
  24.8 25.2 %collective-permute-done.above_hbm = bf16[64,8,256]{2,1,0:T(8,128)(2,1)S(1)} collective-permute-done((bf16[64,8,256]{2,1,0:T(8,128)(2,1)S(1)}, bf16[64,8,256]{2,1,0:T(8,128)(2,1)S(1)}, u32[]{:S(2)}, u32[]{:S(2)}) %collective-permute-start) | collective-permute-done | bytes 262176 | tf_op jit(solution)/shard_map/ppermute | solution.py:400
  50.0 0.0 copy-start.2
  50.0 0.0 collective-permute-done.1.below_hbm
  50.0 0.0 copy-start.3
  50.0 0.0 all-to-all-done.moved_hbm
  50.0 0.0 copy-start.1
  50.1 0.7 copy-done.2
  50.7 0.1 copy-done.3
  50.8 0.4 copy-done.1
  51.3 14.4 %main.1 = (bf16[64,4,8,256]{3,2,1,0:T(8,128)(2,1)}, bf16[1536,256]{1,0:T(8,128)(2,1)}, f32[1536,256]{1,0:T(8,128)}) custom-call(s32[1,6]{1,0:T(1,128)} %lengths_ref.3, s32[1,3]{1,0:T(1,128)} %add_convert_fusion.place_ref, bf16[32,9,8,256]{3,2,1,0:T(8,128)(2,1)} %copy-done.1, bf16[64,4,8,256]{3,2,1,0:T(8,128)(2,1)} %bitcast.44, ...), custom_call_target="tpu_custom_call" | custom-call | tf_op jit(solution)/shard_map/main/pallas_call | solution.py:410
  65.7 0.1 collective-permute-start.2
  65.8 2.5 %collective-permute-done.2 = bf16[1536,256]{1,0:T(8,128)(2,1)S(1)} collective-permute-done((bf16[1536,256]{1,0:T(8,128)(2,1)}, bf16[1536,256]{1,0:T(8,128)(2,1)S(1)}, u32[]{:S(2)}, u32[]{:S(2)}) %collective-permute-start.2) | collective-permute-done | bytes 786464 | tf_op jit(solution)/shard_map/ppermute | solution.py:459
  68.3 1.6 %convert_add_fusion = f32[1536,256]{1,0:T(8,128)S(1)} fusion(f32[1536,256]{1,0:T(8,128)} %get-tuple-element.15, bf16[1536,256]{1,0:T(8,128)(2,1)S(1)} %collective-permute-done.2), kind=kLoop, calls=%fused_computation | loop fusion | flops 786432 | bytes 3932160 | tf_op jit(solution)/shard_map/add | solution.py:459
  69.9 0.1 fusion
  69.9 1.7 %collective-permute-start.3 = (bf16[768,256]{1,0:T(8,128)(2,1)S(1)}, bf16[768,256]{1,0:T(8,128)(2,1)S(1)}, u32[]{:S(2)}, u32[]{:S(2)}) collective-permute-start(bf16[768,256]{1,0:T(8,128)(2,1)S(1)} %fusion), channel_id=1, source_target_pairs={{0,64},{64,0},{128,192},{192,128},{96,160},{160,96},{224,32},{32,2... | collective-permute-start | bytes 1179656 | tf_op jit(solution)/shard_map/ppermute | solution.py:472
  71.6 6.2 %collective-permute-done.3 = bf16[768,256]{1,0:T(8,128)(2,1)S(1)} collective-permute-done((bf16[768,256]{1,0:T(8,128)(2,1)S(1)}, bf16[768,256]{1,0:T(8,128)(2,1)S(1)}, u32[]{:S(2)}, u32[]{:S(2)}) %collective-permute-start.3) | collective-permute-done | bytes 393248 | tf_op jit(solution)/shard_map/ppermute | solution.py:472
  77.8 0.1 bitcast_add_fusion
  77.9 3.1 %collective-permute-start.4 = (bf16[384,256]{1,0:T(8,128)(2,1)S(1)}, bf16[384,256]{1,0:T(8,128)(2,1)S(1)}, u32[]{:S(2)}, u32[]{:S(2)}) collective-permute-start(bf16[384,256]{1,0:T(8,128)(2,1)S(1)} %fusion.1), channel_id=1, source_target_pairs={{64,128},{128,64},{192,0},{0,192},{32,96},{96,32},{160,224},{224,1... | collective-permute-start | bytes 589832 | tf_op jit(solution)/shard_map/ppermute | solution.py:472
  81.0 3.9 %collective-permute-done.4 = bf16[384,256]{1,0:T(8,128)(2,1)S(1)} collective-permute-done((bf16[384,256]{1,0:T(8,128)(2,1)S(1)}, bf16[384,256]{1,0:T(8,128)(2,1)S(1)}, u32[]{:S(2)}, u32[]{:S(2)}) %collective-permute-start.4) | collective-permute-done | bytes 196640 | tf_op jit(solution)/shard_map/ppermute | solution.py:472
  84.9 2.5 %collective-permute-start.5 = (bf16[96,256]{1,0:T(8,128)(2,1)S(1)}, bf16[96,256]{1,0:T(8,128)(2,1)S(1)}, u32[]{:S(2)}, u32[]{:S(2)}) collective-permute-start(bf16[96,256]{1,0:T(8,128)(2,1)S(1)} %get-tuple-element.19), channel_id=1, source_target_pairs={{0,16},{8,24},{16,0},{24,8},{1,17},{9,25},{17,1},{25,9},{2,18},{10... | collective-permute-start | bytes 147464 | tf_op jit(solution)/shard_map/ppermute | solution.py:480
  87.4 1.1 collective-permute-start.7
  88.6 0.9 collective-permute-start.6
  89.5 1.2 collective-permute-done.5
  90.6 0.9 collective-permute-done.7
  91.5 1.1 collective-permute-done.6
  92.7 16.2 %all_to_all.20 = bf16[8,96,256]{2,1,0:T(8,128)(2,1)S(1)} all-to-all(bf16[8,96,256]{2,1,0:T(8,128)(2,1)S(1)} %broadcast_in_dim.10), channel_id=1, replica_groups=mesh['row'=4,'core'=2,'tile_0'=4,'tile_1'=8] {'tile_1'}, dimensions={0} | all-to-all | bytes 786432 | tf_op jit(solution)/shard_map/all_to_all | solution.py:351
  108.9 0.1 reduce_sum.12
  109.0 0.1 broadcast_in_dim.22
  109.1 16.6 %all_to_all.21 = bf16[16,96,256]{2,1,0:T(8,128)(2,1)S(1)} all-to-all(bf16[16,96,256]{2,1,0:T(8,128)(2,1)S(1)} %broadcast_in_dim.22), channel_id=1, replica_groups=mesh['row'=4,'core'=2,'tile_0'=4,'tile_1'=8] {'row','tile_0'}, dimensions={0} | all-to-all | bytes 1572864 | tf_op jit(solution)/shard_map/all_to_all | solution.py:351
  125.7 5.1 %all-to-all-start.1 = ((bf16[32,2,4,8,256]{4,3,2,1,0:T(8,128)(2,1)}), bf16[32,2,4,8,256]{4,3,2,1,0:T(8,128)(2,1)S(1)}, u32[]{:S(2)}, u32[]{:S(2)}) async-start(bf16[32,2,4,8,256]{4,3,2,1,0:T(8,128)(2,1)} %bitcast.8), calls=%async_computation.1 | async-start | bytes 2097152 | tf_op jit(solution)/shard_map/all_to_all | solution.py:351
  130.8 0.0 copy-start
  130.8 0.1 collective-permute-start.8
  130.9 19.8 %all-to-all-done.1 = bf16[32,2,4,8,256]{4,3,2,1,0:T(8,128)(2,1)S(1)} async-done(((bf16[32,2,4,8,256]{4,3,2,1,0:T(8,128)(2,1)}), bf16[32,2,4,8,256]{4,3,2,1,0:T(8,128)(2,1)S(1)}, u32[]{:S(2)}, u32[]{:S(2)}) %all-to-all-start.1) | async-done | bytes 1048608 | tf_op jit(solution)/shard_map/all_to_all | solution.py:351
  150.8 1.1 copy.11
  151.8 0.0 collective-permute-done.8.facing_ref
  151.8 0.0 copy-done
  151.8 2.4 %finish.1 = (f32[2304,256]{1,0:T(8,128)}, f32[768,256]{1,0:T(8,128)}) custom-call(s32[1,3]{1,0:T(1,128)S(1)} %copy-done, bf16[1536,256]{1,0:T(8,128)(2,1)S(1)} %bitcast.40, bf16[1536,256]{1,0:T(8,128)(2,1)S(1)} %collective-permute-done.8.facing_ref), custom_call_target="tpu_custom_call" | custom-call | tf_op jit(solution)/shard_map/finish/pallas_call | solution.py:485
  (5 shorter events, 0.1 us)
Async XLA Ops:
  4.4 11.8 %copy-start.5 = (bf16[64,8,256]{2,1,0:T(8,128)(2,1)S(1)}, bf16[64,8,256]{2,1,0:T(8,128)(2,1)}, u32[]{:S(2)}) copy-start(bf16[64,8,256]{2,1,0:T(8,128)(2,1)} %get-tuple-element.12) | copy-start | bytes 786436
  4.5 15.2 %copy-start.4 = (bf16[64,8,256]{2,1,0:T(8,128)(2,1)S(1)}, bf16[64,8,256]{2,1,0:T(8,128)(2,1)}, u32[]{:S(2)}) copy-start(bf16[64,8,256]{2,1,0:T(8,128)(2,1)} %get-tuple-element.13) | copy-start | bytes 786436
  4.5 45.6 %all-to-all-start = ((bf16[32,9,8,256]{3,2,1,0:T(8,128)(2,1)}), bf16[32,9,8,256]{3,2,1,0:T(8,128)(2,1)S(1)}, u32[]{:S(2)}, u32[]{:S(2)}) async-start(bf16[32,9,8,256]{3,2,1,0:T(8,128)(2,1)} %get-tuple-element.11), calls=%async_computation | async-start | bytes 2359296 | tf_op jit(solution)/shard_map/all_to_all | solution.py:351
  16.2 33.8 %collective-permute-start = (bf16[64,8,256]{2,1,0:T(8,128)(2,1)S(1)}, bf16[64,8,256]{2,1,0:T(8,128)(2,1)S(1)}, u32[]{:S(2)}, u32[]{:S(2)}) collective-permute-start(bf16[64,8,256]{2,1,0:T(8,128)(2,1)S(1)} %copy-done.5), channel_id=1, source_target_pairs={{0,1},{1,2},{2,3},{3,4},{4,5},{5,6},{6,7},{7,8},{8,9},{9,10},{10,1... | collective-permute-start | bytes 786440 | tf_op jit(solution)/shard_map/ppermute | solution.py:400
  19.6 30.4 %collective-permute-start.1 = (bf16[64,8,256]{2,1,0:T(8,128)(2,1)S(1)}, bf16[64,8,256]{2,1,0:T(8,128)(2,1)S(1)}, u32[]{:S(2)}, u32[]{:S(2)}) collective-permute-start(bf16[64,8,256]{2,1,0:T(8,128)(2,1)S(1)} %copy-done.4), channel_id=1, source_target_pairs={{1,0},{2,1},{3,2},{4,3},{5,4},{6,5},{7,6},{8,7},{9,8},{10,9},{11,1... | collective-permute-start | bytes 786440 | tf_op jit(solution)/shard_map/ppermute | solution.py:401
  50.0 0.7 copy-start.2
  50.0 0.8 copy-start.3
  50.0 1.2 copy-start.1
  65.7 2.6 %collective-permute-start.2 = (bf16[1536,256]{1,0:T(8,128)(2,1)}, bf16[1536,256]{1,0:T(8,128)(2,1)S(1)}, u32[]{:S(2)}, u32[]{:S(2)}) collective-permute-start(bf16[1536,256]{1,0:T(8,128)(2,1)} %get-tuple-element.16), channel_id=1, source_target_pairs={{0,32},{32,0},{1,33},{33,1},{2,34},{34,2},{3,35},{35,3},{4,36},{36... | collective-permute-start | bytes 2359304 | tf_op jit(solution)/shard_map/ppermute | solution.py:459
  69.9 7.9 %collective-permute-start.3 = (bf16[768,256]{1,0:T(8,128)(2,1)S(1)}, bf16[768,256]{1,0:T(8,128)(2,1)S(1)}, u32[]{:S(2)}, u32[]{:S(2)}) collective-permute-start(bf16[768,256]{1,0:T(8,128)(2,1)S(1)} %fusion), channel_id=1, source_target_pairs={{0,64},{64,0},{128,192},{192,128},{96,160},{160,96},{224,32},{32,2... | collective-permute-start | bytes 1179656 | tf_op jit(solution)/shard_map/ppermute | solution.py:472
  77.9 7.0 %collective-permute-start.4 = (bf16[384,256]{1,0:T(8,128)(2,1)S(1)}, bf16[384,256]{1,0:T(8,128)(2,1)S(1)}, u32[]{:S(2)}, u32[]{:S(2)}) collective-permute-start(bf16[384,256]{1,0:T(8,128)(2,1)S(1)} %fusion.1), channel_id=1, source_target_pairs={{64,128},{128,64},{192,0},{0,192},{32,96},{96,32},{160,224},{224,1... | collective-permute-start | bytes 589832 | tf_op jit(solution)/shard_map/ppermute | solution.py:472
  84.9 5.7 %collective-permute-start.5 = (bf16[96,256]{1,0:T(8,128)(2,1)S(1)}, bf16[96,256]{1,0:T(8,128)(2,1)S(1)}, u32[]{:S(2)}, u32[]{:S(2)}) collective-permute-start(bf16[96,256]{1,0:T(8,128)(2,1)S(1)} %get-tuple-element.19), channel_id=1, source_target_pairs={{0,16},{8,24},{16,0},{24,8},{1,17},{9,25},{17,1},{25,9},{2,18},{10... | collective-permute-start | bytes 147464 | tf_op jit(solution)/shard_map/ppermute | solution.py:480
  87.4 4.1 %collective-permute-start.7 = (bf16[96,256]{1,0:T(8,128)(2,1)S(1)}, bf16[96,256]{1,0:T(8,128)(2,1)S(1)}, u32[]{:S(2)}, u32[]{:S(2)}) collective-permute-start(bf16[96,256]{1,0:T(8,128)(2,1)S(1)} %get-tuple-element.20), channel_id=1, source_target_pairs={{0,24},{8,0},{16,8},{24,16},{1,25},{9,1},{17,9},{25,17},{2,26},{10... | collective-permute-start | bytes 147464 | tf_op jit(solution)/shard_map/ppermute | solution.py:480
  88.6 4.1 %collective-permute-start.6 = (bf16[96,256]{1,0:T(8,128)(2,1)S(1)}, bf16[96,256]{1,0:T(8,128)(2,1)S(1)}, u32[]{:S(2)}, u32[]{:S(2)}) collective-permute-start(bf16[96,256]{1,0:T(8,128)(2,1)S(1)} %get-tuple-element.21), channel_id=1, source_target_pairs={{0,8},{8,16},{16,24},{24,0},{1,9},{9,17},{17,25},{25,1},{2,10},{10... | collective-permute-start | bytes 147464 | tf_op jit(solution)/shard_map/ppermute | solution.py:480
  125.7 25.0 %all-to-all-start.1 = ((bf16[32,2,4,8,256]{4,3,2,1,0:T(8,128)(2,1)}), bf16[32,2,4,8,256]{4,3,2,1,0:T(8,128)(2,1)S(1)}, u32[]{:S(2)}, u32[]{:S(2)}) async-start(bf16[32,2,4,8,256]{4,3,2,1,0:T(8,128)(2,1)} %bitcast.8), calls=%async_computation.1 | async-start | bytes 2097152 | tf_op jit(solution)/shard_map/all_to_all | solution.py:351
  130.8 21.0 %copy-start = (s32[1,3]{1,0:T(1,128)S(1)}, s32[1,3]{1,0:T(1,128)}, u32[]{:S(2)}) copy-start(s32[1,3]{1,0:T(1,128)} %add_convert_fusion.place_ref) | copy-start | bytes 40
  130.8 21.0 %collective-permute-start.8 = (bf16[1536,256]{1,0:T(8,128)(2,1)S(1)}, bf16[1536,256]{1,0:T(8,128)(2,1)S(1)}, u32[]{:S(2)}, u32[]{:S(2)}) collective-permute-start(bf16[1536,256]{1,0:T(8,128)(2,1)S(1)} %bitcast.39), channel_id=1, source_target_pairs={{0,32},{32,0},{1,33},{33,1},{2,34},{34,2},{3,35},{35,3},{4,36},{36... | collective-permute-start | bytes 2359304 | tf_op jit(solution)/shard_map/ppermute | solution.py:484
